TPU v7x, 256 devices: a whole 4x4x8 slice. The times are simulated.
256 devices in a mesh: sec: 16 (over x, y_hi, core), span: 16 (over z, y_lo).
Axes of the slice: x: 4, y: 4 (y_hi: 2, y_lo: 2; y = y_hi * 2 + y_lo), z: 8, core: 2. Of those that a mesh axis runs over, the one named last changes fastest.
Arguments:
- density: float32 [384, 4096], P('sec', 'span'), may hold values from 0.5 to 2
- fields: float32 [4, 384, 4096], P(None, 'sec', 'span'), may hold values from -6 to 6
- bins: int32 [384, 4096], P('sec', 'span'), may hold values from 0 to 127
- owner: int32 [384], P('sec'), may hold values from 0 to 255
- species: float32 [256, 32, 128], P(('sec', 'span')), may hold values from -6 to 6
- rate_matrix: float32 [32, 32], replicated, may hold values from -1 to 1
- inv_weight: float32 [32], replicated, may hold values from 0.5 to 2
- formation: float32 [32], replicated, may hold values from -4 to 4
Outputs:
- species_out: float32 [256, 32, 128], P(('sec', 'span'))
- density_out: float32 [384, 4096], P('sec', 'span')
- fields_out: float32 [4, 384, 4096], P(None, 'sec', 'span')
All inputs are finite; a program needn't handle non-finite values.
Results may differ from a plain program's by a relative error of at most 0.0003.
Values sent between devices are 32-bit elements; how exact they have to be, the bound alone decides.
No kernel may reach another device: no remote copies, remote signals or barrier semaphores. Data moves between devices by JAX's collectives and lax.ppermute only.
A program may use at most 64 MiB of HBM per device.

v0:
```python
import math

import jax
import jax.numpy as jnp
from jax import lax
from jax.sharding import PartitionSpec as P

COUPLING = 2


def from_behind(value, axis, steps):
    count = lax.axis_size(axis)
    first, last = (max(0, -steps), min(count, count - steps))
    return lax.ppermute(value, axis, [(source, source + steps) for source in range(first, last)])


def extended_2(shard, sides, width):
    for axis, dim in sides:
        count, length = (lax.axis_size(axis), shard.shape[dim])
        up = [(i, (i + 1) % count) for i in range(count)]
        down = [(j, i) for i, j in up]
        last = lax.slice_in_dim(shard, length - width, length, axis=dim)
        first = lax.slice_in_dim(shard, 0, width, axis=dim)
        before = lax.ppermute(last, axis, up)
        after = lax.ppermute(first, axis, down)
        shard = jnp.concatenate([before, shard, after], axis=dim)
    return shard


def column_sums(values, bins, nbins):
    cols, quant, zlen = values.shape
    block = math.gcd(cols, 16)
    value_blocks = values.reshape(cols // block, block, quant, zlen)
    bin_blocks = bins.reshape(cols // block, block, zlen)

    def one_block(pair):
        vals, labels = pair
        hot = (labels[:, :, None] == jnp.arange(nbins, dtype=jnp.int32)).astype(jnp.float32)
        return jnp.einsum("cqz,czb->cqb", vals, hot, precision=lax.Precision.HIGHEST)

    out = lax.map(one_block, (value_blocks, bin_blocks))
    return out.reshape(cols, quant * nbins)


def body(density, fields, bins, owner, species, rate_matrix, inv_weight, formation):
    nbins = species.shape[2]
    nspec = species.shape[1]
    sections = lax.axis_size("sec") * lax.axis_size("span")
    mine = lax.axis_index("sec") * lax.axis_size("span") + lax.axis_index("span")
    eta = (jnp.arange(nbins, dtype=jnp.float32) + 0.5) / nbins
    index = owner[:, None] * nbins + bins
    for step in range(COUPLING):
        values = jnp.stack([density] + [density * fields[k] for k in range(4)], axis=1)
        hist = column_sums(values, bins, nbins)
        hot = (owner[:, None] == jnp.arange(sections, dtype=jnp.int32)[None, :]).astype(jnp.float32)
        total = lax.psum(
            lax.dot_general(
                hot,
                hist,
                (((0,), (0,)), ((), ())),
                precision=lax.Precision.HIGHEST,
                preferred_element_type=jnp.float32,
            ),
            ("sec", "span"),
        )
        own = lax.dynamic_slice_in_dim(total, mine, 1, 0)
        own = own.reshape(5, nbins)
        weight = jnp.maximum(own[0], 1.0)
        cond = own[1:] / weight[None]
        current = species[0]
        before = from_behind(species, ("sec", "span"), 1)[0]
        temp = 1.0 + 4.0 * eta * (1.0 - eta) + 0.5 * jnp.tanh(cond[2])
        rate = jnp.exp(2.0 * (1.0 - 1.0 / temp))
        react = (
            jnp.dot(
                rate_matrix,
                current,
                precision=lax.Precision.HIGHEST,
                preferred_element_type=jnp.float32,
            )
            * rate[None, :]
        )
        padded = jnp.pad(current, ((0, 0), (1, 1)))
        lap = padded[:, 2:] + padded[:, :-2] - 2.0 * current
        mixing = 0.2 * jax.nn.sigmoid(cond[1])
        carried = 0.3 * jax.nn.sigmoid(cond[0])
        updated = (
            current + mixing[None, :] * lap - carried[None, :] * (current - before) + 0.2 * react
        )
        species = updated[None]
        mix = 1.0 + jnp.sum(inv_weight[:, None] * updated * updated, axis=0) / nspec
        rho_c = 1.0 / (temp * mix)
        temp_c = (
            temp
            + 0.1 * jnp.sum(formation[:, None] * react, axis=0)
            - 0.2 * jax.nn.sigmoid(cond[3]) * (temp - 0.5)
        )
        table = jnp.stack([rho_c, temp_c])[None]
        whole = lax.all_gather(table, ("sec", "span"), axis=0, tiled=True)
        rho_cell = whole[:, 0, :].reshape(-1)[index]
        temp_cell = whole[:, 1, :].reshape(-1)[index]
        extended = extended_2(fields, (("span", 2),), 1)
        lapz = extended[:, :, 2:] + extended[:, :, :-2] - 2.0 * fields
        fields = fields + 0.2 * lapz
        fields = fields.at[2].add(0.3 * (temp_cell - fields[2]))
        density = rho_cell
    return (species, density, fields)


def solution(mesh):
    return jax.shard_map(
        body,
        mesh=mesh,
        in_specs=(
            P("sec", "span"),
            P(None, "sec", "span"),
            P("sec", "span"),
            P("sec"),
            P(("sec", "span"), None, None),
            P(),
            P(),
            P(),
        ),
        out_specs=(P(("sec", "span"), None, None), P("sec", "span"), P(None, "sec", "span")),
        check_vma=False,
    )
```

profile of v0, /device:TPU:1, one launch (start us, length us, event | category | flops | bytes accessed | tf_op | source)
XLA Modules:
  0.0 1891.0 jit_solution(5151774485042406274)
XLA Ops:
  7.2 0.8 stack.38
  8.1 0.8 bitcast_multiply_fusion
  9.2 0.7 copy-done.2
  10.0 2.4 while.22
  10.0 0.8 fusion.68
  10.8 0.8 fusion.68
  11.6 0.8 fusion.68
  13.1 1.4 fusion.21
  15.2 4.0 collective-permute-start
  19.3 5.3 collective-permute-start.1
  24.7 1.1 collective-permute-done.1
  25.8 3.9 collective-permute-done.2
  29.8 243.0 %all-reduce.5.cloned.1.call-done = f32[256,640]{1,0:T(8,128)} async-done(((f32[256,640]{1,0:T(8,128)}), f32[256,640]{1,0:T(8,128)}) %all-reduce.5.cloned.1.call-update) | async-done | bytes 655376 | tf_op jit(solution)/shard_map/psum | solution.py:56
  272.8 0.7 fusion.46
  273.5 0.8 dynamic-slice.16
  275.2 593.2 %all-gather.2 = f32[256,2,128]{2,1,0:T(2,128)S(1)} all-gather(f32[1,2,128]{2,1,0:T(2,128)S(1)} %maximum_bitcast_fusion), channel_id=2, replica_groups=mesh['sec'=16,'span'=16] {'sec','span'}, dimensions={0}, use_global_device_ids=true | all-gather | bytes 263168 | tf_op jit(solution)/shard_map/all_gather | solution.py:99
  868.6 34.3 %gather_fusion.1 = f32[6144]{0:T(1024)S(1)} fusion(f32[32768]{0:T(1024)S(1)} %bitcast.132, s32[6144]{0:T(1024)S(1)} %broadcast_clamp_fusion), kind=kCustom, calls=%fused_computation.1 | custom fusion | bytes 73728 | tf_op jit(solution)/shard_map/gather | solution.py:101
  902.9 34.3 %gather_fusion = f32[6144]{0:T(1024)S(1)} fusion(f32[32768]{0:T(1024)S(1)} %bitcast.130, s32[6144]{0:T(1024)S(1)} %broadcast_clamp_fusion), kind=kCustom, calls=%fused_computation | custom fusion | bytes 73728 | tf_op jit(solution)/shard_map/gather | solution.py:100
  937.6 2.5 while.23
  937.6 0.8 fusion.70
  938.4 0.8 fusion.70
  939.2 0.8 fusion.70
  940.1 1.4 fusion.18
  941.6 1.5 collective-permute-start.5
  943.0 1.9 collective-permute-start.3
  945.0 1.7 collective-permute-done.5
  946.9 271.6 %all-reduce.7.cloned.1.call-done = f32[256,640]{1,0:T(8,128)} async-done(((f32[256,640]{1,0:T(8,128)}), f32[256,640]{1,0:T(8,128)}) %all-reduce.7.cloned.1.call-update) | async-done | bytes 655376 | tf_op jit(solution)/shard_map/psum | solution.py:56
  1219.1 0.8 dynamic-slice.18
  1220.2 0.7 fusion.26
  1220.9 593.2 %all-gather.3 = f32[256,2,128]{2,1,0:T(2,128)S(1)} all-gather(f32[1,2,128]{2,1,0:T(2,128)S(1)} %maximum_bitcast_fusion.1), channel_id=3, replica_groups=mesh['sec'=16,'span'=16] {'sec','span'}, dimensions={0}, use_global_device_ids=true | all-gather | bytes 263168 | tf_op jit(solution)/shard_map/all_gather | solution.py:99
  1814.3 34.3 %gather_fusion.3 = f32[6144]{0:T(1024)S(1)} fusion(f32[32768]{0:T(1024)S(1)} %bitcast.133, s32[6144]{0:T(1024)S(1)} %broadcast_clamp_fusion), kind=kCustom, calls=%fused_computation.3 | custom fusion | bytes 73728 | tf_op jit(solution)/shard_map/gather | solution.py:101
  1848.6 34.3 %gather_fusion.2 = f32[6144]{0:T(1024)S(1)} fusion(f32[32768]{0:T(1024)S(1)} %bitcast.131, s32[6144]{0:T(1024)S(1)} %broadcast_clamp_fusion), kind=kCustom, calls=%fused_computation.2 | custom fusion | bytes 73728 | tf_op jit(solution)/shard_map/gather | solution.py:100
  (68 shorter events, 6.1 us)
Async XLA Ops:
  7.2 267.2 %copy-start = (f32[32,32]{1,0:T(8,128)S(1)}, f32[32,32]{1,0:T(8,128)}, u32[]{:S(2)}) copy-start(f32[32,32]{1,0:T(8,128)} %param.21) | copy-start | bytes 12292
  7.2 265.6 %all-reduce.5.cloned.1.call-start = ((), (), s32[]{:S(2)}) async-start(), calls=%async_computation | async-start | bytes 1310720 | tf_op jit(solution)/shard_map/psum | solution.py:56
  7.2 0.8 copy-start.4
  9.2 0.7 copy-start.2
  12.4 0.7 copy-start.5
  14.5 0.7 copy-start.7
  14.5 4.7 copy-start.1
  14.5 1204.0 %all-reduce.7.cloned.1.call-start = ((), (), s32[]{:S(2)}) async-start(), calls=%async_computation.1 | async-start | bytes 1310720 | tf_op jit(solution)/shard_map/psum | solution.py:56
  15.2 259.1 %collective-permute-start = (f32[1,32,128]{2,1,0:T(8,128)S(1)}, f32[1,32,128]{2,1,0:T(8,128)S(1)}, u32[]{:S(2)}, u32[]{:S(2)}) collective-permute-start(f32[1,32,128]{2,1,0:T(8,128)S(1)} %copy-done.7), channel_id=1, source_target_pairs={{0,1},{1,2},{2,3},{3,4},{4,5},{5,6},{6,7},{7,8},{8,9},{9,10},{10,1... | collective-permute-start | bytes 49160 | tf_op jit(solution)/shard_map/ppermute | solution.py:14
  19.3 6.5 collective-permute-start.1
  24.6 5.0 collective-permute-start.2
  274.3 0.7 copy-start.6
  274.3 0.7 copy-start.8
  941.6 3.4 collective-permute-start.4
  941.6 5.1 collective-permute-start.5
  943.0 277.1 %collective-permute-start.3 = (f32[1,32,128]{2,1,0:T(8,128)S(1)}, f32[1,32,128]{2,1,0:T(8,128)S(1)}, u32[]{:S(2)}, u32[]{:S(2)}) collective-permute-start(f32[1,32,128]{2,1,0:T(8,128)S(1)} %bitcast.139), channel_id=1, source_target_pairs={{0,1},{1,2},{2,3},{3,4},{4,5},{5,6},{6,7},{7,8},{8,9},{9,10},{10,1... | collective-permute-start | bytes 49160 | tf_op jit(solution)/shard_map/ppermute | solution.py:14
  1883.5 0.6 copy-start.3
Sparse Core Ops, SparseCore 0:
  14.6 258.1 all-reduce.4
  941.6 276.8 all-reduce.6
where the time goes:
time: 1920 us; the launch traced here: 1890 us
  blocking collectives  1190 us (62%)
  waiting for transfers between devices  521 us (27%)
  local copies, waits for them, and re-layouts  145 us (8%)
    all_gather x2, blocking collectives, body(): whole = lax.all_gather(table, ('sec', 'span'), axis=0, tiled=True)  1190 us
    psum x2, waiting for transfers between devices, body(): lax.psum(lax.dot_general(hot, hist, (((0,), (0,)), ((), ())), precision=l...  515 us
    gather x3, local copies, waits for them, and re-layouts, body(): rho_cell = whole[:, 0, :].reshape(-1)[index]  69.2 us
    gather x4, local copies, waits for them, and re-layouts, body(): temp_cell = whole[:, 1, :].reshape(-1)[index]  68.6 us
  transfers between devices with their start and end apart: 8, of which 5 were waited for; matrix products, arithmetic and copies ran while one was open for 0% of the time, Pallas kernels for 0%

commit v1 on v0

v1 whole, which is shorter than its diff:
```python
import jax
import jax.numpy as jnp
from jax import lax
from jax.experimental import pallas as pl
from jax.experimental.pallas import tpu as pltpu
from jax.sharding import PartitionSpec as P

F32, BF16 = jnp.float32, jnp.bfloat16
C, Z, NB, NS = 24, 256, 128, 32
G = 16
SECT = 256
LF, LC, LH, LE = 0, 32, 40, 90
LB0, LB1, LOWN = 106, 107, 108
R1 = 32
R2 = C + 3 * G


def iota(shape, dim):
    return lax.broadcasted_iota(jnp.int32, shape, dim)


def parts(value):
    high = value.astype(BF16)
    rest = value - high.astype(F32)
    mid = rest.astype(BF16)
    low = (rest - mid.astype(F32)).astype(BF16)
    return high, mid, low


def column_of(row, n):
    return jnp.sum(jnp.where(iota((n, n), 0) == iota((n, n), 1), row, 0.0), axis=1, keepdims=True)


def sigmoid(x):
    return 0.5 * jnp.tanh(0.5 * x) + 0.5


def dot(a, b, dims):
    return lax.dot_general(a, b, (dims, ((), ())), preferred_element_type=F32)


def bin_kernel(den, fields, bins, owner, species, out, vals, hist, turned, rows):
    lane = iota((C, Z), 1)
    d = den[...]
    vals[0] = d
    vals[5] = jnp.ones((C, Z), F32)
    for k in range(4):
        f = fields[k]
        left = jnp.where(lane == 0, 0.0, pltpu.roll(f, 1, 1))
        right = jnp.where(lane == Z - 1, 0.0, pltpu.roll(f, Z - 1, 1))
        vals[1 + k] = d * f
        vals[6 + k] = f + 0.2 * (left + right - 2.0 * f)
    for q in range(10, 16):
        vals[q] = jnp.zeros((C, Z), F32)
    which = iota((NB, Z), 0)
    for c in range(C):
        hot = jnp.where(which == bins[c : c + 1, :], 1.0, 0.0).astype(BF16)
        full = dot(jnp.concatenate(parts(vals[:, c, :]), axis=0), hot, ((1,), (1,)))
        hist[c] = full[0:16] + full[16:32] + full[32:48]
    lane = iota((C, NB), 1)
    edge = jnp.zeros((C, NB), F32)
    for k in range(4):
        first, last = fields[k, :, 0:NB], fields[k, :, Z - NB : Z]
        for e, (tile, at) in enumerate(((first, 0), (first, 1), (last, NB - 2), (last, NB - 1))):
            to = LE + 4 * e + k
            edge = jnp.where(lane == to, pltpu.roll(tile, (to - at) % NB, 1), edge)
    first, last = bins[:, 0:NB].astype(F32), bins[:, Z - NB : Z].astype(F32)
    edge = jnp.where(lane == LB0, pltpu.roll(first, LB0, 1), edge)
    edge = jnp.where(lane == LB1, pltpu.roll(last, (LB1 + 1) % NB, 1), edge)
    edge = jnp.where(lane == LOWN, column_of(owner[...].astype(F32), C), edge)
    sums = [hist[:, q, :] for q in range(10)]
    turned[0:8, :] = jnp.zeros((8, NB), F32)
    turned[8 + NB : 16 + NB, :] = jnp.zeros((8, NB), F32)
    turned[8 : 8 + NB, :] = jnp.concatenate([species[0], jnp.zeros((NB - NS, NB), F32)], axis=0).T
    packed = turned[pl.ds(6, 33, stride=4), :]
    for a in range(1, 4):
        packed = packed + pltpu.roll(turned[pl.ds(6 + a, 33, stride=4), :], 32 * a, 1)
    rows[0:33, :] = packed
    rows[33:40, :] = jnp.zeros((7, NB), F32)
    for dest in range(G):
        acc = edge
        for k in range(4):
            start = LF + 8 * k
            moved = pltpu.roll(sums[6 + k], (start - 8 * dest) % NB, 1)
            acc = jnp.where((lane >= start) & (lane < start + 8), moved, acc)
        moved = pltpu.roll(sums[5], (LC - 8 * dest) % NB, 1)
        acc = jnp.where((lane >= LC) & (lane < LC + 8), moved, acc)
        for q in range(5):
            start = LH + 10 * q
            moved = pltpu.roll(sums[q], (start - 8 * dest + 1) % NB, 1)
            acc = jnp.where((lane >= start) & (lane < start + 10), moved, acc)
        out[dest, 0:C, :] = acc
        out[dest, C:R1, :] = rows[2 * dest : 2 * dest + 8, :]


def column_kernel(got, out, halo):
    me = lax.axis_index("span")
    lane = iota((C, NB), 1)
    total = got[0, 0:C, :]
    for j in range(1, G):
        total = total + got[j, 0:C, :]
    source, to = iota((NB, 2 * NB), 0), iota((NB, 2 * NB), 1)
    pick = jnp.where(
        to < 32,
        LE + 12 + to // 8,
        jnp.where(
            to < 64,
            LE + (to - 32) // 8,
            jnp.where((to >= 128) & (to < 160), LB0, jnp.where((to >= 160) & (to < 192), LB1, -1)),
        ),
    )
    spread = jnp.where(source == pick, 1.0, 0.0).astype(BF16)
    wide = got[:, 0:C, :].reshape(G * C, NB)
    high, mid, low = parts(wide)
    moved = dot(high, spread, ((1,), (0,))) + dot(mid, spread, ((1,), (0,))) + dot(low, spread, ((1,), (0,)))
    bin_here = (8 * me + lane % 8).astype(F32)
    part = [moved[C * j : C * (j + 1), 0:NB] for j in range(G)]
    fix = jnp.zeros((C, NB), F32)
    for j in range(G):
        beside = jnp.where(lane < 32, part[(j - 1) % G], part[(j + 1) % G])
        fix = fix + jnp.where(moved[C * j : C * (j + 1), NB : 2 * NB] == bin_here, beside, 0.0)
    fix = fix + pltpu.roll(fix, NB - 32, 1)
    total = total + jnp.where(lane < 32, 0.2 * fix, 0.0)
    total = jnp.where(lane >= LE, got[0, 0:C, :], total)
    tiles = [got[:, C + t, :] for t in range(3)]
    for i in range(G):
        out[i, 0:C, :] = total
        for t in range(3):
            out[i, C + G * t : C + G * (t + 1), :] = tiles[t]
    halo[0] = got[lax.rem(me + G - 1, G), 0:C, :]
    halo[1] = got[lax.rem(me + 1, G), 0:C, :]


def section_kernel(got, rate_matrix, inv_weight, formation, out, sums, turned):
    row_at, me = lax.axis_index("sec"), lax.axis_index("span")
    wide = got[:, 0:C, :].reshape(G * C, NB)
    section = iota((G * C, SECT), 1).astype(F32)
    hot = jnp.where(wide[:, LOWN : LOWN + 1] == section, 1.0, 0.0).astype(BF16)
    full = dot(jnp.concatenate(parts(wide.T), axis=0), hot, ((1,), (0,)))
    sums[...] = full[0:NB] + full[NB : 2 * NB] + full[2 * NB : 3 * NB]
    weights = column_of(inv_weight[...], NS)
    heats = column_of(formation[...], NS)
    block = jnp.concatenate([rate_matrix[...]] * 4, axis=1)
    block = jnp.concatenate([block] * 4, axis=0)
    block = jnp.where(iota((NB, NB), 0) // NS == iota((NB, NB), 1) // NS, block, 0.0)
    first_lane = iota((NS, SECT), 1) == 0

    def rates(tile):
        return jnp.dot(block, tile, precision=lax.Precision.HIGHEST, preferred_element_type=F32)

    def advance(density, moments, bin_at, current, reaction):
        n = density.shape[0]
        weight = jnp.maximum(density, 1.0)
        cond = [m / weight for m in moments]
        eta = ((bin_at + iota((n, SECT), 0)).astype(F32) + 0.5) / NB
        temp = 1.0 + 4.0 * eta * (1.0 - eta) + 0.5 * jnp.tanh(cond[2])
        rate = jnp.exp(2.0 * (1.0 - 1.0 / temp))
        mixing = 0.2 * sigmoid(cond[1])
        carried = 0.3 * sigmoid(cond[0])
        updated, mixes, released = [], [], []
        for r in range(n):
            here = current[r + 1]
            before = jnp.where(first_lane, 0.0, pltpu.roll(here, 1, 1))
            react = reaction[r] * rate[r : r + 1]
            new = (
                here
                + mixing[r : r + 1] * (current[r + 2] + current[r] - 2.0 * here)
                - carried[r : r + 1] * (here - before)
                + 0.2 * react
            )
            updated.append(new)
            mixes.append(jnp.sum(weights * new * new, axis=0, keepdims=True))
            released.append(jnp.sum(heats * react, axis=0, keepdims=True))
        mix = 1.0 + jnp.concatenate(mixes, axis=0) / NS
        rho = 1.0 / (temp * mix)
        temp_c = temp + 0.1 * jnp.concatenate(released, axis=0) - 0.2 * sigmoid(cond[3]) * (temp - 0.5)
        return updated, rho, temp_c

    tiles = [got[:, C + G * t : C + G * (t + 1), :].reshape(SECT, NB).T for t in range(3)]
    reacts = [rates(tile) for tile in tiles]
    current = [tiles[b // 4][NS * (b % 4) : NS * (b % 4 + 1)] for b in range(12)]
    reaction = [reacts[b // 4][NS * (b % 4) : NS * (b % 4 + 1)] for b in range(1, 11)]
    first = [sums[LH + 10 * q : LH + 10 * (q + 1), :] for q in range(5)]
    updated, rho, temp0 = advance(first[0], first[1:], 8 * me - 1, current, reaction)
    updated[0] = jnp.where(me == 0, 0.0, updated[0])
    updated[9] = jnp.where(me == G - 1, 0.0, updated[9])
    rho, temp0 = rho[1:9], temp0[1:9]
    count = sums[LC : LC + 8, :]
    moments = [rho * sums[LF + 8 * k : LF + 8 * k + 8, :] for k in range(4)]
    moments[2] = 0.7 * moments[2] + 0.3 * rho * temp0 * count
    reacts = [rates(jnp.concatenate(updated[1 + 4 * t : 5 + 4 * t], axis=0)) for t in range(2)]
    reaction = [reacts[b // 4][NS * (b % 4) : NS * (b % 4 + 1)] for b in range(8)]
    final, rho, temp1 = advance(rho * count, moments, 8 * me, updated, reaction)

    own = got[row_at, 0:C, LOWN : LOWN + 1]
    own = jnp.concatenate([own] * 3 + [jnp.full((NB - 3 * C, 1), -1.0, F32)], axis=0)
    hot = jnp.where(own == iota((NB, SECT), 1).astype(F32), 1.0, 0.0).astype(BF16)
    table = jnp.concatenate([temp0, temp1, rho], axis=0)
    full = dot(jnp.concatenate(parts(table), axis=0), hot, ((1,), (1,)))
    full = full[0:24] + full[24:48] + full[48:72]
    lane = iota((8, NB), 1)
    cells = jnp.where(lane < C, full[0:8], jnp.where(lane < 2 * C, full[8:16], full[16:24]))
    for t in range(2):
        tile = jnp.concatenate(final[4 * t : 4 * t + 4], axis=0)
        turned[t] = jnp.where(row_at < 8, tile[:, 0:NB], tile[:, NB:SECT]).T
    lane = iota((G, NB), 1)
    start = pl.multiple_of(16 * lax.rem(row_at, 8), 16)
    for b in range(8):
        own_sections = turned[b // 4, pl.ds(start, G), :]
        moved = pltpu.roll(own_sections, (96 - 32 * (b % 4)) % NB, 1)
        out[:, b, :] = jnp.where(lane >= 96, moved, cells[b : b + 1, :])


def cell_kernel(got, halo, fields, bins, species_out, density_out, fields_out):
    table = got[...].reshape(NB, NB).T
    species_out[0] = table[96:128]
    temp0, temp1, rho = table[0:C], table[C : 2 * C], table[2 * C : 3 * C]

    def look(tab, index):
        return jnp.take_along_axis(tab, index, axis=1)

    def cells(tab):
        return jnp.concatenate([look(tab, bins[:, 0:NB]), look(tab, bins[:, NB:Z])], axis=1)

    density_out[...] = cells(rho)
    lane = iota((C, Z), 1)
    left, right = halo[0], halo[1]

    def shifted(f, before, after):
        return jnp.where(lane == 0, before, pltpu.roll(f, 1, 1)) + jnp.where(
            lane == Z - 1, after, pltpu.roll(f, Z - 1, 1)
        )

    for k in range(4):
        f = fields[k]
        l1, l2 = left[:, LE + 12 + k : LE + 13 + k], left[:, LE + 8 + k : LE + 9 + k]
        r1, r2 = right[:, LE + k : LE + 1 + k], right[:, LE + 4 + k : LE + 5 + k]
        new = f + 0.2 * (shifted(f, l1, r1) - 2.0 * f)
        new_l = l1 + 0.2 * (l2 + f[:, 0:1] - 2.0 * l1)
        new_r = r1 + 0.2 * (f[:, Z - 1 : Z] + r2 - 2.0 * r1)
        if k == 2:
            new = new + 0.3 * (cells(temp0) - new)
            at_l = jnp.broadcast_to(left[:, LB1 : LB1 + 1].astype(jnp.int32), (C, NB))
            at_r = jnp.broadcast_to(right[:, LB0 : LB0 + 1].astype(jnp.int32), (C, NB))
            new_l = new_l + 0.3 * (look(temp0, at_l)[:, 0:1] - new_l)
            new_r = new_r + 0.3 * (look(temp0, at_r)[:, 0:1] - new_r)
        new = new + 0.2 * (shifted(new, new_l, new_r) - 2.0 * new)
        if k == 2:
            new = new + 0.3 * (cells(temp1) - new)
        fields_out[k] = new


def call(kernel, name, outs, ins, scratch=()):
    space = pl.BlockSpec(memory_space=pltpu.VMEM)
    shapes = [jax.ShapeDtypeStruct(s, F32) for s in outs]
    return pl.pallas_call(
        kernel,
        name=name,
        out_shape=shapes,
        in_specs=[space] * len(ins),
        out_specs=[space] * len(outs),
        scratch_shapes=[pltpu.VMEM(s, F32) for s in scratch],
    )(*ins)


def body(density, fields, bins, owner, species, rate_matrix, inv_weight, formation):
    (sent,) = call(
        bin_kernel,
        "bin",
        [(G, R1, NB)],
        [density, fields, bins, owner.reshape(1, C), species],
        [(16, C, Z), (C, 16, NB), (16 + NB, NB), (40, NB)],
    )
    got = lax.all_to_all(sent, "span", 0, 0, tiled=True)
    sent, halo = call(column_kernel, "column", [(G, R2, NB), (2, C, NB)], [got])
    got = lax.all_to_all(sent, "sec", 0, 0, tiled=True)
    (sent,) = call(
        section_kernel,
        "section",
        [(G, 8, NB)],
        [got, rate_matrix, inv_weight.reshape(1, NS), formation.reshape(1, NS)],
        [(NB, SECT), (2, NB, NB)],
    )
    got = lax.all_to_all(sent, "span", 0, 0, tiled=True)
    return call(
        cell_kernel,
        "cell",
        [(1, NS, NB), (C, Z), (4, C, Z)],
        [got, halo, fields, bins],
    )


def solution(mesh):
    return jax.shard_map(
        lambda *args: tuple(body(*args)),
        mesh=mesh,
        in_specs=(
            P("sec", "span"),
            P(None, "sec", "span"),
            P("sec", "span"),
            P("sec"),
            P(("sec", "span"), None, None),
            P(),
            P(),
            P(),
        ),
        out_specs=(P(("sec", "span"), None, None), P("sec", "span"), P(None, "sec", "span")),
        check_vma=False,
    )
```

time: 1920 us -> 68 us (0.04); the launches traced: 1890 us -> 67.5 us
  blocking collectives: 1190 us -> 54.8 us
  waiting for transfers between devices: 521 us -> 0 us
  local copies, waits for them, and re-layouts: 145 us -> 0 us
    all_gather x2 -> x0, blocking collectives: 1190 us -> none  [body(): whole = lax.all_gather(table, ('sec', 'span'), axis=0, tiled=True)]
    psum x2 -> x0, waiting for transfers between devices: 515 us -> none  [body(): lax.psum(lax.dot_general(hot, hist, (((0,), (0,)), ((), ())), precision=l...]
    gather x7 -> x0, local copies, waits for them, and re-layouts: 138 us -> none  [the longest x3 69.2 us: body(): rho_cell = whole[:, 0, :].reshape(-1)[index]]
    all_to_all x0 -> x3, blocking collectives: none -> 54.8 us  [the longest x2 32.9 us: body(): got = lax.all_to_all(sent, 'span', 0, 0, tiled=True)]
  transfers between devices with their start and end apart: 8 -> 0, of which waited for: 5 -> 0; matrix products, arithmetic and copies ran while one was open for 0% -> 0% of each run, Pallas kernels for 0% -> 0%
where the time goes in v1:
time: 68 us; the launch traced here: 67.5 us
  blocking collectives  54.8 us (81%)
  Pallas kernels  12.1 us (18%)
    all_to_all x2, blocking collectives, body(): got = lax.all_to_all(sent, 'span', 0, 0, tiled=True)  32.9 us
    all_to_all x1, blocking collectives, body(): got = lax.all_to_all(sent, 'sec', 0, 0, tiled=True)  21.9 us
    pallas_call x4, Pallas kernels, call(): pl.pallas_call(kernel, name=name, out_shape=shapes, in_specs=[space] * le...  12.1 us

profile of v1, /device:TPU:1, one launch (start us, length us, event | category | flops | bytes accessed | tf_op | source)
XLA Modules:
  0.0 67.5 jit_solution(1153394029502773369)
XLA Ops:
  0.6 4.4 %bin.1 = f32[16,32,128]{2,1,0:T(8,128)} custom-call(f32[24,256]{1,0:T(8,128)} %den.1, f32[4,24,256]{2,1,0:T(8,128)} %fields.3, s32[24,256]{1,0:T(8,128)} %bins.3, s32[1,24]{1,0:T(1,128)} %bitcast.3, f32[1,32,128]{2,1,0:T(8,128)} %species.1), custom_call_target="tpu_custom_call" | custom-call | tf_op jit(solution)/shard_map/bin/pallas_call | solution.py:256
  5.0 20.8 %all_to_all.15.got = f32[16,32,128]{2,1,0:T(8,128)} all-to-all(f32[16,32,128]{2,1,0:T(8,128)} %bin.1), channel_id=1, replica_groups=mesh['sec'=16,'span'=16] {'span'}, dimensions={0} | all-to-all | bytes 524288 | tf_op jit(solution)/shard_map/all_to_all | solution.py:274
  25.8 2.2 %column.1 = (f32[16,72,128]{2,1,0:T(8,128)}, f32[2,24,128]{2,1,0:T(8,128)}) custom-call(f32[16,32,128]{2,1,0:T(8,128)} %all_to_all.15.got), custom_call_target="tpu_custom_call" | custom-call | tf_op jit(solution)/shard_map/column/pallas_call | solution.py:256
  28.0 21.9 %all_to_all.16.got = f32[16,72,128]{2,1,0:T(8,128)} all-to-all(f32[16,72,128]{2,1,0:T(8,128)} %get-tuple-element.5), channel_id=1, replica_groups=mesh['sec'=16,'span'=16] {'sec'}, dimensions={0} | all-to-all | bytes 1179648 | tf_op jit(solution)/shard_map/all_to_all | solution.py:276
  49.9 3.0 %section.1 = f32[16,8,128]{2,1,0:T(8,128)} custom-call(f32[16,72,128]{2,1,0:T(8,128)} %all_to_all.16.got, f32[32,32]{1,0:T(8,128)} %rate_matrix.1, f32[1,32]{1,0:T(1,128)} %bitcast.4, f32[1,32]{1,0:T(1,128)} %bitcast.5), custom_call_target="tpu_custom_call" | custom-call | tf_op jit(solution)/shard_map/section/pallas_call | solution.py:256
  52.9 12.1 %all_to_all.17.got = f32[16,8,128]{2,1,0:T(8,128)} all-to-all(f32[16,8,128]{2,1,0:T(8,128)} %section.1), channel_id=1, replica_groups=mesh['sec'=16,'span'=16] {'span'}, dimensions={0} | all-to-all | bytes 131072 | tf_op jit(solution)/shard_map/all_to_all | solution.py:284
  65.0 2.5 %cell.1 = (f32[1,32,128]{2,1,0:T(8,128)}, f32[24,256]{1,0:T(8,128)}, f32[4,24,256]{2,1,0:T(8,128)}) custom-call(f32[16,8,128]{2,1,0:T(8,128)} %all_to_all.17.got, f32[2,24,128]{2,1,0:T(8,128)} %get-tuple-element.6.halo, f32[4,24,256]{2,1,0:T(8,128)} %fields.3, s32[24,256]{1,0:T(8,128)} %bins.3), custom_call_target="tpu_custom_call" | custom-call | tf_op jit(solution)/shard_map/cell/pallas_call | solution.py:256

commit v2 on v1

--- a/solution.py
+++ b/solution.py
@@ -11,7 +11,7 @@
 SECT = 256
 LF, LC, LH, LE = 0, 32, 40, 90
 LB0, LB1, LOWN = 106, 107, 108
-R1 = 32
+LS = 112
 R2 = C + 3 * G
 
 
@@ -39,7 +39,14 @@
     return lax.dot_general(a, b, (dims, ((), ())), preferred_element_type=F32)
 
 
-def bin_kernel(den, fields, bins, owner, species, out, vals, hist, turned, rows):
+def bin_kernel(*refs):
+    out, vals, hist, rows = refs[5:9]
+    den, fields, bins, owner, species = refs[9:14]
+    copies = [pltpu.make_async_copy(refs[n], refs[9 + n], refs[14].at[n]) for n in range(5)]
+    for copy in copies:
+        copy.start()
+    for copy in copies:
+        copy.wait()
     lane = iota((C, Z), 1)
     d = den[...]
     vals[0] = d
@@ -69,16 +76,13 @@
     edge = jnp.where(lane == LB1, pltpu.roll(last, (LB1 + 1) % NB, 1), edge)
     edge = jnp.where(lane == LOWN, column_of(owner[...].astype(F32), C), edge)
     sums = [hist[:, q, :] for q in range(10)]
-    turned[0:8, :] = jnp.zeros((8, NB), F32)
-    turned[8 + NB : 16 + NB, :] = jnp.zeros((8, NB), F32)
-    turned[8 : 8 + NB, :] = jnp.concatenate([species[0], jnp.zeros((NB - NS, NB), F32)], axis=0).T
-    packed = turned[pl.ds(6, 33, stride=4), :]
-    for a in range(1, 4):
-        packed = packed + pltpu.roll(turned[pl.ds(6 + a, 33, stride=4), :], 32 * a, 1)
-    rows[0:33, :] = packed
-    rows[33:40, :] = jnp.zeros((7, NB), F32)
+    turned = jnp.concatenate([species[0], jnp.zeros((NB - NS, NB), F32)], axis=0).T
+    rows[0:8, :] = jnp.zeros((8, NB), F32)
+    rows[256:264, :] = jnp.zeros((8, NB), F32)
+    rows[pl.ds(4, NB, stride=2), :] = pltpu.roll(turned, LS, 1)
+    rows[pl.ds(5, NB, stride=2), :] = pltpu.roll(turned, LS - 16, 1)
     for dest in range(G):
-        acc = edge
+        acc = jnp.where(lane >= LS, rows[16 * dest : 16 * dest + C, :], edge)
         for k in range(4):
             start = LF + 8 * k
             moved = pltpu.roll(sums[6 + k], (start - 8 * dest) % NB, 1)
@@ -89,8 +93,7 @@
             start = LH + 10 * q
             moved = pltpu.roll(sums[q], (start - 8 * dest + 1) % NB, 1)
             acc = jnp.where((lane >= start) & (lane < start + 10), moved, acc)
-        out[dest, 0:C, :] = acc
-        out[dest, C:R1, :] = rows[2 * dest : 2 * dest + 8, :]
+        out[dest] = acc
 
 
 def column_kernel(got, out, halo):
@@ -122,8 +125,15 @@
     fix = fix + pltpu.roll(fix, NB - 32, 1)
     total = total + jnp.where(lane < 32, 0.2 * fix, 0.0)
     total = jnp.where(lane >= LE, got[0, 0:C, :], total)
-    tiles = [got[:, C + t, :] for t in range(3)]
-    for i in range(G):
+    lane = iota((G, NB), 1)
+    tiles = []
+    for t in range(3):
+        tile = jnp.zeros((G, NB), F32)
+        for p in range(8):
+            moved = pltpu.roll(got[:, 8 * t + p, :], (16 * p - LS) % NB, 1)
+            tile = jnp.where((lane >= 16 * p) & (lane < 16 * p + 16), moved, tile)
+        tiles.append(tile)
+    for i in range(G // 2):
         out[i, 0:C, :] = total
         for t in range(3):
             out[i, C + G * t : C + G * (t + 1), :] = tiles[t]
@@ -131,9 +141,10 @@
     halo[1] = got[lax.rem(me + 1, G), 0:C, :]
 
 
-def section_kernel(got, rate_matrix, inv_weight, formation, out, sums, turned):
+def section_kernel(got, other, rate_matrix, inv_weight, formation, out, sums, turned):
     row_at, me = lax.axis_index("sec"), lax.axis_index("span")
-    wide = got[:, 0:C, :].reshape(G * C, NB)
+    half = G // 2 * C
+    wide = jnp.concatenate([got[:, 0:C, :].reshape(half, NB), other[:, 0:C, :].reshape(half, NB)], axis=0)
     section = iota((G * C, SECT), 1).astype(F32)
     hot = jnp.where(wide[:, LOWN : LOWN + 1] == section, 1.0, 0.0).astype(BF16)
     full = dot(jnp.concatenate(parts(wide.T), axis=0), hot, ((1,), (0,)))
@@ -176,7 +187,15 @@
         temp_c = temp + 0.1 * jnp.concatenate(released, axis=0) - 0.2 * sigmoid(cond[3]) * (temp - 0.5)
         return updated, rho, temp_c
 
-    tiles = [got[:, C + G * t : C + G * (t + 1), :].reshape(SECT, NB).T for t in range(3)]
+    even = lax.rem(row_at, 2) == 0
+    tiles = []
+    for t in range(3):
+        span = slice(C + G * t, C + G * (t + 1))
+        tile = []
+        for i in range(G):
+            mine, theirs = got[i // 2, span, :], other[i // 2, span, :]
+            tile.append(jnp.where(even, mine, theirs) if i % 2 == 0 else jnp.where(even, theirs, mine))
+        tiles.append(jnp.concatenate(tile, axis=0).T)
     reacts = [rates(tile) for tile in tiles]
     current = [tiles[b // 4][NS * (b % 4) : NS * (b % 4 + 1)] for b in range(12)]
     reaction = [reacts[b // 4][NS * (b % 4) : NS * (b % 4 + 1)] for b in range(1, 11)]
@@ -192,7 +211,7 @@
     reaction = [reacts[b // 4][NS * (b % 4) : NS * (b % 4 + 1)] for b in range(8)]
     final, rho, temp1 = advance(rho * count, moments, 8 * me, updated, reaction)
 
-    own = got[row_at, 0:C, LOWN : LOWN + 1]
+    own = got[row_at // 2, 0:C, LOWN : LOWN + 1]
     own = jnp.concatenate([own] * 3 + [jnp.full((NB - 3 * C, 1), -1.0, F32)], axis=0)
     hot = jnp.where(own == iota((NB, SECT), 1).astype(F32), 1.0, 0.0).astype(BF16)
     table = jnp.concatenate([temp0, temp1, rho], axis=0)
@@ -250,35 +269,33 @@
         fields_out[k] = new
 
 
-def call(kernel, name, outs, ins, scratch=()):
-    space = pl.BlockSpec(memory_space=pltpu.VMEM)
-    shapes = [jax.ShapeDtypeStruct(s, F32) for s in outs]
+def call(kernel, name, outs, ins, scratch=(), space=pltpu.VMEM):
     return pl.pallas_call(
         kernel,
         name=name,
-        out_shape=shapes,
-        in_specs=[space] * len(ins),
-        out_specs=[space] * len(outs),
-        scratch_shapes=[pltpu.VMEM(s, F32) for s in scratch],
+        out_shape=[jax.ShapeDtypeStruct(s, F32) for s in outs],
+        in_specs=[pl.BlockSpec(memory_space=space)] * len(ins),
+        out_specs=[pl.BlockSpec(memory_space=pltpu.VMEM)] * len(outs),
+        scratch_shapes=[pltpu.VMEM(s, F32) if isinstance(s, tuple) else s for s in scratch],
+        compiler_params=pltpu.CompilerParams(vmem_limit_bytes=16 << 20),
     )(*ins)
 
 
 def body(density, fields, bins, owner, species, rate_matrix, inv_weight, formation):
-    (sent,) = call(
-        bin_kernel,
-        "bin",
-        [(G, R1, NB)],
-        [density, fields, bins, owner.reshape(1, C), species],
-        [(16, C, Z), (C, 16, NB), (16 + NB, NB), (40, NB)],
-    )
+    ins = [density, fields, bins, owner.reshape(1, C), species]
+    scratch = [(16, C, Z), (C, 16, NB), (264, NB)]
+    scratch += [pltpu.VMEM(x.shape, x.dtype) for x in ins] + [pltpu.SemaphoreType.DMA((5,))]
+    (sent,) = call(bin_kernel, "bin", [(G, C, NB)], ins, scratch, pltpu.HBM)
     got = lax.all_to_all(sent, "span", 0, 0, tiled=True)
-    sent, halo = call(column_kernel, "column", [(G, R2, NB), (2, C, NB)], [got])
-    got = lax.all_to_all(sent, "sec", 0, 0, tiled=True)
+    sent, halo = call(column_kernel, "column", [(G // 2, R2, NB), (2, C, NB)], [got])
+    groups = [list(range(core, G, 2)) for core in range(2)]
+    got = lax.all_to_all(sent, "sec", 0, 0, axis_index_groups=groups, tiled=True)
+    other = lax.ppermute(got, "sec", [(i, i ^ 1) for i in range(G)])
     (sent,) = call(
         section_kernel,
         "section",
         [(G, 8, NB)],
-        [got, rate_matrix, inv_weight.reshape(1, NS), formation.reshape(1, NS)],
+        [got, other, rate_matrix, inv_weight.reshape(1, NS), formation.reshape(1, NS)],
         [(NB, SECT), (2, NB, NB)],
     )
     got = lax.all_to_all(sent, "span", 0, 0, tiled=True)

time: 68 us -> 61.1 us (0.90)
  blocking collectives: 54.8 us -> 44.1 us
  Pallas kernels: 12.1 us -> 6.38 us
  local copies, waits for them, and re-layouts: 0 us -> 4.42 us
  starting transfers between devices: 0 us -> 3.89 us
  waiting for transfers between devices: 0 us -> 1.21 us
    all_to_all x1, blocking collectives: 21.9 us -> 14.1 us  [body(): lax.all_to_all(sent, 'sec', 0, 0, axis_index_groups=groups, tiled=True)]
    pallas_call x4, Pallas kernels: 12.1 us -> 6.38 us  [call(): pl.pallas_call(kernel, name=name, out_shape=[jax.ShapeDtypeStruct(s, F32)...]
    unnamed x0 -> x20, local copies, waits for them, and re-layouts: none -> 4.42 us
    ppermute x0 -> x1, starting transfers between devices: none -> 3.89 us  [body(): other = lax.ppermute(got, 'sec', [(i, i ^ 1) for i in range(G)])]
    all_to_all x2, blocking collectives: 32.9 us -> 30 us  [body(): got = lax.all_to_all(sent, 'span', 0, 0, tiled=True)]
    ppermute x0 -> x1, waiting for transfers between devices: none -> 1.21 us  [body(): other = lax.ppermute(got, 'sec', [(i, i ^ 1) for i in range(G)])]
  transfers between devices with their start and end apart: 0 -> 1, of which waited for: 0 -> 1; matrix products, arithmetic and copies ran while one was open for 0% -> 0% of each run, Pallas kernels for 0% -> 0%
where the time goes in v2:
time: 61.1 us; the launch traced here: 60.7 us
  blocking collectives  44.1 us (72%)
  Pallas kernels  6.38 us (10%)
  local copies, waits for them, and re-layouts  4.42 us (7%)
  starting transfers between devices  3.89 us (6%)
  waiting for transfers between devices  1.21 us (2%)
  between operations  0.7 us (1%)
    all_to_all x2, blocking collectives, body(): got = lax.all_to_all(sent, 'span', 0, 0, tiled=True)  30 us
    all_to_all x1, blocking collectives, body(): lax.all_to_all(sent, 'sec', 0, 0, axis_index_groups=groups, tiled=True)  14.1 us
    pallas_call x4, Pallas kernels, call(): pl.pallas_call(kernel, name=name, out_shape=[jax.ShapeDtypeStruct(s, F32)...  6.38 us
    unnamed x20, local copies, waits for them, and re-layouts  4.42 us
    ppermute x1, starting transfers between devices, body(): other = lax.ppermute(got, 'sec', [(i, i ^ 1) for i in range(G)])  3.89 us
  transfers between devices with their start and end apart: 1, of which 1 were waited for; matrix products, arithmetic and copies ran while one was open for 0% of the time, Pallas kernels for 0%

profile of v2, /device:TPU:1, one launch (start us, length us, event | category | flops | bytes accessed | tf_op | source)
XLA Modules:
  0.0 60.7 jit_solution(13559146824953447011)
XLA Ops:
  0.6 0.0 copy-start.7
  0.6 0.6 %copy-done.7 = s32[24]{0:T(128)S(1)} copy-done((s32[24]{0:T(128)S(1)}, s32[24]{0:T(128)}, u32[]{:S(2)}) %copy-start.7) | copy-done | bytes 120
  1.3 0.0 copy-start
  1.3 0.9 %copy-done = f32[4,24,256]{2,1,0:T(8,128)S(1)} copy-done((f32[4,24,256]{2,1,0:T(8,128)S(1)}, f32[4,24,256]{2,1,0:T(8,128)}, u32[]{:S(2)}) %copy-start) | copy-done | bytes 98328
  2.2 0.0 copy-start.2
  2.2 0.7 %copy-done.2 = s32[24,256]{1,0:T(8,128)S(1)} copy-done((s32[24,256]{1,0:T(8,128)S(1)}, s32[24,256]{1,0:T(8,128)}, u32[]{:S(2)}) %copy-start.2) | copy-done | bytes 24600
  2.9 0.0 copy-start.4
  2.9 0.7 %copy-done.4 = f32[24,256]{1,0:T(8,128)S(1)} copy-done((f32[24,256]{1,0:T(8,128)S(1)}, f32[24,256]{1,0:T(8,128)}, u32[]{:S(2)}) %copy-start.4) | copy-done | bytes 24600
  3.7 0.0 copy-start.5
  3.7 0.7 %copy-done.5 = f32[1,32,128]{2,1,0:T(8,128)S(1)} copy-done((f32[1,32,128]{2,1,0:T(8,128)S(1)}, f32[1,32,128]{2,1,0:T(8,128)}, u32[]{:S(2)}) %copy-start.5) | copy-done | bytes 16408
  4.4 3.1 %bin.1 = f32[16,24,128]{2,1,0:T(8,128)S(1)} custom-call(f32[24,256]{1,0:T(8,128)S(1)} %copy-done.4, f32[4,24,256]{2,1,0:T(8,128)S(1)} %copy-done, s32[24,256]{1,0:T(8,128)S(1)} %copy-done.2, s32[1,24]{1,0:T(1,128)S(1)} %bitcast.3, f32[1,32,128]{2,1,0:T(8,128)S(1)} %copy-done.5), custom_call_target="tpu_custom_call" | custom-call | tf_op jit(solution)/shard_map/bin/pallas_call | solution.py:273
  7.4 19.3 %all_to_all.15.got = f32[16,24,128]{2,1,0:T(8,128)S(1)} all-to-all(f32[16,24,128]{2,1,0:T(8,128)S(1)} %bin.1), channel_id=1, replica_groups=mesh['sec'=16,'span'=16] {'span'}, dimensions={0} | all-to-all | bytes 393216 | tf_op jit(solution)/shard_map/all_to_all | solution.py:289
  26.7 0.4 column.1
  27.2 0.0 copy-start.6
  27.2 14.1 %all_to_all.16.got = f32[8,72,128]{2,1,0:T(8,128)S(1)} all-to-all(f32[8,72,128]{2,1,0:T(8,128)S(1)} %get-tuple-element.5), channel_id=1, replica_groups={{0,32,64,96,128,160,192,224},{16,48,80,112,144,176,208,240},{1,33,65,97..., dimensions={0} | all-to-all | bytes 589824 | tf_op jit(solution)/shard_map/all_to_all | solution.py:292
  41.3 3.9 %collective-permute-start = (f32[8,72,128]{2,1,0:T(8,128)S(1)}, f32[8,72,128]{2,1,0:T(8,128)S(1)}, u32[]{:S(2)}, u32[]{:S(2)}) collective-permute-start(f32[8,72,128]{2,1,0:T(8,128)S(1)} %all_to_all.16.got), channel_id=1, source_target_pairs={{0,16},{16,0},{32,48},{48,32},{64,80},{80,64},{96,112},{112,96},{1... | collective-permute-start | bytes 884744 | tf_op jit(solution)/shard_map/ppermute | solution.py:293
  45.2 1.2 %collective-permute-done.other = f32[8,72,128]{2,1,0:T(8,128)S(1)} collective-permute-done((f32[8,72,128]{2,1,0:T(8,128)S(1)}, f32[8,72,128]{2,1,0:T(8,128)S(1)}, u32[]{:S(2)}, u32[]{:S(2)}) %collective-permute-start) | collective-permute-done | bytes 294944 | tf_op jit(solution)/shard_map/ppermute | solution.py:293
  46.4 0.0 copy-start.8
  46.4 0.0 copy-start.9
  46.4 0.0 copy-done.6
  46.4 0.6 %copy-done.8 = f32[32]{0:T(128)S(1)} copy-done((f32[32]{0:T(128)S(1)}, f32[32]{0:T(128)}, u32[]{:S(2)}) %copy-start.8) | copy-done | bytes 152
  47.0 0.0 copy-done.9
  47.1 1.3 %section.1 = f32[16,8,128]{2,1,0:T(8,128)S(1)} custom-call(f32[8,72,128]{2,1,0:T(8,128)S(1)} %all_to_all.16.got, f32[8,72,128]{2,1,0:T(8,128)S(1)} %collective-permute-done.other, f32[32,32]{1,0:T(8,128)S(1)} %copy-done.6, f32[1,32]{1,0:T(1,128)S(1)} %bitcast.4, f32[1,32]{1,0:T(1,128)S(1)} %bitcast.5), custom_call_target="tpu_custom_call" | custom-call | tf_op jit(solution)/shard_map/section/pallas_call | solution.py:273
  48.4 0.0 copy-start.1
  48.4 0.0 copy-start.3
  48.4 10.7 %all_to_all.17.got = f32[16,8,128]{2,1,0:T(8,128)S(1)} all-to-all(f32[16,8,128]{2,1,0:T(8,128)S(1)} %section.1), channel_id=1, replica_groups=mesh['sec'=16,'span'=16] {'span'}, dimensions={0} | all-to-all | bytes 131072 | tf_op jit(solution)/shard_map/all_to_all | solution.py:301
  59.1 0.0 copy-done.1
  59.1 0.0 copy-done.3
  59.1 1.6 %cell.1 = (f32[1,32,128]{2,1,0:T(8,128)}, f32[24,256]{1,0:T(8,128)}, f32[4,24,256]{2,1,0:T(8,128)}) custom-call(f32[16,8,128]{2,1,0:T(8,128)S(1)} %all_to_all.17.got, f32[2,24,128]{2,1,0:T(8,128)S(1)} %get-tuple-element.6.halo, f32[4,24,256]{2,1,0:T(8,128)S(1)} %copy-done.1, s32[24,256]{1,0:T(8,128)S(1)} %copy-done.3), custom_call_target="tpu_custom_call" | custom-call | tf_op jit(solution)/shard_map/cell/pallas_call | solution.py:273
Async XLA Ops:
  0.6 0.7 %copy-start.7 = (s32[24]{0:T(128)S(1)}, s32[24]{0:T(128)}, u32[]{:S(2)}) copy-start(s32[24]{0:T(128)} %param.11) | copy-start | bytes 292
  1.3 0.9 %copy-start = (f32[4,24,256]{2,1,0:T(8,128)S(1)}, f32[4,24,256]{2,1,0:T(8,128)}, u32[]{:S(2)}) copy-start(f32[4,24,256]{2,1,0:T(8,128)} %fields.1) | copy-start | bytes 294916
  2.2 0.7 %copy-start.2 = (s32[24,256]{1,0:T(8,128)S(1)}, s32[24,256]{1,0:T(8,128)}, u32[]{:S(2)}) copy-start(s32[24,256]{1,0:T(8,128)} %bins.1) | copy-start | bytes 73732
  2.9 0.7 %copy-start.4 = (f32[24,256]{1,0:T(8,128)S(1)}, f32[24,256]{1,0:T(8,128)}, u32[]{:S(2)}) copy-start(f32[24,256]{1,0:T(8,128)} %refs_0_.1) | copy-start | bytes 73732
  3.7 0.7 %copy-start.5 = (f32[1,32,128]{2,1,0:T(8,128)S(1)}, f32[1,32,128]{2,1,0:T(8,128)}, u32[]{:S(2)}) copy-start(f32[1,32,128]{2,1,0:T(8,128)} %refs_4_.1) | copy-start | bytes 49156
  27.2 19.2 %copy-start.6 = (f32[32,32]{1,0:T(8,128)S(1)}, f32[32,32]{1,0:T(8,128)}, u32[]{:S(2)}) copy-start(f32[32,32]{1,0:T(8,128)} %rate_matrix.1) | copy-start | bytes 12292
  41.3 5.1 %collective-permute-start = (f32[8,72,128]{2,1,0:T(8,128)S(1)}, f32[8,72,128]{2,1,0:T(8,128)S(1)}, u32[]{:S(2)}, u32[]{:S(2)}) collective-permute-start(f32[8,72,128]{2,1,0:T(8,128)S(1)} %all_to_all.16.got), channel_id=1, source_target_pairs={{0,16},{16,0},{32,48},{48,32},{64,80},{80,64},{96,112},{112,96},{1... | collective-permute-start | bytes 884744 | tf_op jit(solution)/shard_map/ppermute | solution.py:293
  46.4 0.7 %copy-start.8 = (f32[32]{0:T(128)S(1)}, f32[32]{0:T(128)}, u32[]{:S(2)}) copy-start(f32[32]{0:T(128)} %param.14) | copy-start | bytes 388
  46.4 0.7 %copy-start.9 = (f32[32]{0:T(128)S(1)}, f32[32]{0:T(128)}, u32[]{:S(2)}) copy-start(f32[32]{0:T(128)} %param.15) | copy-start | bytes 388
  48.4 10.7 %copy-start.1 = (f32[4,24,256]{2,1,0:T(8,128)S(1)}, f32[4,24,256]{2,1,0:T(8,128)}, u32[]{:S(2)}) copy-start(f32[4,24,256]{2,1,0:T(8,128)} %fields.1) | copy-start | bytes 294916
  48.4 10.7 %copy-start.3 = (s32[24,256]{1,0:T(8,128)S(1)}, s32[24,256]{1,0:T(8,128)}, u32[]{:S(2)}) copy-start(s32[24,256]{1,0:T(8,128)} %bins.1) | copy-start | bytes 73732

commit v3 on v2

--- a/solution.py
+++ b/solution.py
@@ -40,30 +40,52 @@
 
 
 def bin_kernel(*refs):
-    out, vals, hist, rows = refs[5:9]
-    den, fields, bins, owner, species = refs[9:14]
-    copies = [pltpu.make_async_copy(refs[n], refs[9 + n], refs[14].at[n]) for n in range(5)]
+    ins, (sent, consts), held = refs[0:8], refs[8:10], refs[10:18]
+    vals, hist, rows, labels, out, shared, arrived, left = refs[18:26]
+    bins, fields, den, species, owner, rate_matrix, inv_weight, formation = held
+    copies = [pltpu.make_async_copy(ins[n], held[n], arrived.at[n]) for n in range(8)]
     for copy in copies:
         copy.start()
     for copy in copies:
         copy.wait()
+    lane = iota((NS, NB), 1)
+    block = jnp.concatenate([rate_matrix[...], jnp.zeros((NS, NB - NS), F32)], axis=1)
+    block = jnp.where(lane == NS, column_of(inv_weight[...], NS), block)
+    shared[...] = jnp.where(lane == NS + 1, column_of(formation[...], NS), block)
+    leaving = [pltpu.make_async_copy(shared, consts, left.at[G])]
+    leaving[0].start()
     lane = iota((C, Z), 1)
     d = den[...]
-    vals[0] = d
-    vals[5] = jnp.ones((C, Z), F32)
+
+    def keep(q, value):
+        high, mid, low = parts(value)
+        for p, part in enumerate((high, mid, low)):
+            at = C * (16 * p + q)
+            part = part.astype(F32)
+            vals[0, at : at + C, :] = part[:, 0:NB]
+            vals[1, at : at + C, :] = part[:, NB:Z]
+
+    keep(0, d)
+    keep(5, jnp.ones((C, Z), F32))
     for k in range(4):
         f = fields[k]
-        left = jnp.where(lane == 0, 0.0, pltpu.roll(f, 1, 1))
-        right = jnp.where(lane == Z - 1, 0.0, pltpu.roll(f, Z - 1, 1))
-        vals[1 + k] = d * f
-        vals[6 + k] = f + 0.2 * (left + right - 2.0 * f)
-    for q in range(10, 16):
-        vals[q] = jnp.zeros((C, Z), F32)
-    which = iota((NB, Z), 0)
+        before = jnp.where(lane == 0, 0.0, pltpu.roll(f, 1, 1))
+        after = jnp.where(lane == Z - 1, 0.0, pltpu.roll(f, Z - 1, 1))
+        keep(1 + k, d * f)
+        keep(6 + k, f + 0.2 * (before + after - 2.0 * f))
+    for p in range(3):
+        at = C * (16 * p + 10)
+        for h in range(2):
+            vals[h, at : at + 6 * C, :] = jnp.zeros((6 * C, NB), F32)
+    labels[...] = bins[...].astype(F32)
+    which = iota((NB, Z), 0).astype(F32).astype(BF16).reshape(8, 16, Z)
+    one, zero = jnp.ones((8, 16, Z), BF16), jnp.zeros((8, 16, Z), BF16)
     for c in range(C):
-        hot = jnp.where(which == bins[c : c + 1, :], 1.0, 0.0).astype(BF16)
-        full = dot(jnp.concatenate(parts(vals[:, c, :]), axis=0), hot, ((1,), (1,)))
-        hist[c] = full[0:16] + full[16:32] + full[32:48]
+        label = jnp.broadcast_to(labels[c : c + 1, :], (16, Z)).astype(BF16)
+        hot = jnp.where(which == label[None], one, zero).reshape(NB, Z)
+        cells = [vals[h, pl.ds(c, 48, stride=C), :] for h in range(2)]
+        full = dot(jnp.concatenate(cells, axis=1).astype(BF16), hot, ((1,), (1,)))
+        hist[16 * c : 16 * c + 16, :] = full[0:16] + full[16:32] + full[32:48]
     lane = iota((C, NB), 1)
     edge = jnp.zeros((C, NB), F32)
     for k in range(4):
@@ -71,11 +93,11 @@
         for e, (tile, at) in enumerate(((first, 0), (first, 1), (last, NB - 2), (last, NB - 1))):
             to = LE + 4 * e + k
             edge = jnp.where(lane == to, pltpu.roll(tile, (to - at) % NB, 1), edge)
-    first, last = bins[:, 0:NB].astype(F32), bins[:, Z - NB : Z].astype(F32)
+    first, last = labels[:, 0:NB], labels[:, Z - NB : Z]
     edge = jnp.where(lane == LB0, pltpu.roll(first, LB0, 1), edge)
     edge = jnp.where(lane == LB1, pltpu.roll(last, (LB1 + 1) % NB, 1), edge)
     edge = jnp.where(lane == LOWN, column_of(owner[...].astype(F32), C), edge)
-    sums = [hist[:, q, :] for q in range(10)]
+    sums = [hist[pl.ds(q, C, stride=16), :] for q in range(10)]
     turned = jnp.concatenate([species[0], jnp.zeros((NB - NS, NB), F32)], axis=0).T
     rows[0:8, :] = jnp.zeros((8, NB), F32)
     rows[256:264, :] = jnp.zeros((8, NB), F32)
@@ -94,14 +116,18 @@
             moved = pltpu.roll(sums[q], (start - 8 * dest + 1) % NB, 1)
             acc = jnp.where((lane >= start) & (lane < start + 10), moved, acc)
         out[dest] = acc
+        leaving.append(pltpu.make_async_copy(out.at[dest], sent.at[dest], left.at[dest]))
+        leaving[-1].start()
+    for copy in leaving:
+        copy.wait()
 
 
 def column_kernel(got, out, halo):
     me = lax.axis_index("span")
     lane = iota((C, NB), 1)
-    total = got[0, 0:C, :]
+    total = got[0:C, :]
     for j in range(1, G):
-        total = total + got[j, 0:C, :]
+        total = total + got[C * j : C * (j + 1), :]
     source, to = iota((NB, 2 * NB), 0), iota((NB, 2 * NB), 1)
     pick = jnp.where(
         to < 32,
@@ -113,8 +139,7 @@
         ),
     )
     spread = jnp.where(source == pick, 1.0, 0.0).astype(BF16)
-    wide = got[:, 0:C, :].reshape(G * C, NB)
-    high, mid, low = parts(wide)
+    high, mid, low = parts(got[...])
     moved = dot(high, spread, ((1,), (0,))) + dot(mid, spread, ((1,), (0,))) + dot(low, spread, ((1,), (0,)))
     bin_here = (8 * me + lane % 8).astype(F32)
     part = [moved[C * j : C * (j + 1), 0:NB] for j in range(G)]
@@ -124,24 +149,24 @@
         fix = fix + jnp.where(moved[C * j : C * (j + 1), NB : 2 * NB] == bin_here, beside, 0.0)
     fix = fix + pltpu.roll(fix, NB - 32, 1)
     total = total + jnp.where(lane < 32, 0.2 * fix, 0.0)
-    total = jnp.where(lane >= LE, got[0, 0:C, :], total)
+    total = jnp.where(lane >= LE, got[0:C, :], total)
     lane = iota((G, NB), 1)
     tiles = []
     for t in range(3):
         tile = jnp.zeros((G, NB), F32)
         for p in range(8):
-            moved = pltpu.roll(got[:, 8 * t + p, :], (16 * p - LS) % NB, 1)
+            moved = pltpu.roll(got[pl.ds(8 * t + p, G, stride=C), :], (16 * p - LS) % NB, 1)
             tile = jnp.where((lane >= 16 * p) & (lane < 16 * p + 16), moved, tile)
         tiles.append(tile)
     for i in range(G // 2):
         out[i, 0:C, :] = total
         for t in range(3):
             out[i, C + G * t : C + G * (t + 1), :] = tiles[t]
-    halo[0] = got[lax.rem(me + G - 1, G), 0:C, :]
-    halo[1] = got[lax.rem(me + 1, G), 0:C, :]
-
-
-def section_kernel(got, other, rate_matrix, inv_weight, formation, out, sums, turned):
+    halo[0] = got[pl.ds(pl.multiple_of(C * lax.rem(me + G - 1, G), 8), C), :]
+    halo[1] = got[pl.ds(pl.multiple_of(C * lax.rem(me + 1, G), 8), C), :]
+
+
+def section_kernel(got, other, consts, out, sums, turned):
     row_at, me = lax.axis_index("sec"), lax.axis_index("span")
     half = G // 2 * C
     wide = jnp.concatenate([got[:, 0:C, :].reshape(half, NB), other[:, 0:C, :].reshape(half, NB)], axis=0)
@@ -149,15 +174,18 @@
     hot = jnp.where(wide[:, LOWN : LOWN + 1] == section, 1.0, 0.0).astype(BF16)
     full = dot(jnp.concatenate(parts(wide.T), axis=0), hot, ((1,), (0,)))
     sums[...] = full[0:NB] + full[NB : 2 * NB] + full[2 * NB : 3 * NB]
-    weights = column_of(inv_weight[...], NS)
-    heats = column_of(formation[...], NS)
-    block = jnp.concatenate([rate_matrix[...]] * 4, axis=1)
+    weights, heats = consts[:, NS : NS + 1], consts[:, NS + 1 : NS + 2]
+    block = jnp.concatenate([consts[:, 0:NS]] * 4, axis=1)
     block = jnp.concatenate([block] * 4, axis=0)
     block = jnp.where(iota((NB, NB), 0) // NS == iota((NB, NB), 1) // NS, block, 0.0)
+    high, mid, low = parts(block)
+    blocks = [jnp.concatenate(pair, axis=1) for pair in ((high, mid), (mid, high), (low, high))]
     first_lane = iota((NS, SECT), 1) == 0
 
     def rates(tile):
-        return jnp.dot(block, tile, precision=lax.Precision.HIGHEST, preferred_element_type=F32)
+        high, mid, low = parts(tile)
+        pairs = (high, mid), (high, mid), (high, low)
+        return sum(dot(a, jnp.concatenate(b, axis=0), ((1,), (0,))) for a, b in zip(blocks, pairs))
 
     def advance(density, moments, bin_at, current, reaction):
         n = density.shape[0]
@@ -227,12 +255,19 @@
     for b in range(8):
         own_sections = turned[b // 4, pl.ds(start, G), :]
         moved = pltpu.roll(own_sections, (96 - 32 * (b % 4)) % NB, 1)
-        out[:, b, :] = jnp.where(lane >= 96, moved, cells[b : b + 1, :])
-
-
-def cell_kernel(got, halo, fields, bins, species_out, density_out, fields_out):
+        out[pl.ds(b, G, stride=8), :] = jnp.where(lane >= 96, moved, cells[b : b + 1, :])
+
+
+def cell_kernel(got, halo, fields, bins, species_to, density_to, fields_to, species_out, density_out, fields_out, left_at):
+    leaving = []
+
+    def leave(source, to):
+        leaving.append(pltpu.make_async_copy(source, to, left_at.at[len(leaving)]))
+        leaving[-1].start()
+
     table = got[...].reshape(NB, NB).T
     species_out[0] = table[96:128]
+    leave(species_out, species_to)
     temp0, temp1, rho = table[0:C], table[C : 2 * C], table[2 * C : 3 * C]
 
     def look(tab, index):
@@ -242,6 +277,7 @@
         return jnp.concatenate([look(tab, bins[:, 0:NB]), look(tab, bins[:, NB:Z])], axis=1)
 
     density_out[...] = cells(rho)
+    leave(density_out, density_to)
     lane = iota((C, Z), 1)
     left, right = halo[0], halo[1]
 
@@ -250,7 +286,7 @@
             lane == Z - 1, after, pltpu.roll(f, Z - 1, 1)
         )
 
-    for k in range(4):
+    for k in (2, 0, 1, 3):
         f = fields[k]
         l1, l2 = left[:, LE + 12 + k : LE + 13 + k], left[:, LE + 8 + k : LE + 9 + k]
         r1, r2 = right[:, LE + k : LE + 1 + k], right[:, LE + 4 + k : LE + 5 + k]
@@ -267,44 +303,53 @@
         if k == 2:
             new = new + 0.3 * (cells(temp1) - new)
         fields_out[k] = new
-
-
-def call(kernel, name, outs, ins, scratch=(), space=pltpu.VMEM):
+        leave(fields_out.at[k], fields_to.at[k])
+    for copy in leaving:
+        copy.wait()
+
+
+def call(kernel, name, outs, ins, scratch=(), source=pltpu.VMEM, to=pltpu.VMEM, limit=16 << 20):
     return pl.pallas_call(
         kernel,
         name=name,
         out_shape=[jax.ShapeDtypeStruct(s, F32) for s in outs],
-        in_specs=[pl.BlockSpec(memory_space=space)] * len(ins),
-        out_specs=[pl.BlockSpec(memory_space=pltpu.VMEM)] * len(outs),
+        in_specs=[pl.BlockSpec(memory_space=source)] * len(ins),
+        out_specs=[pl.BlockSpec(memory_space=to)] * len(outs),
         scratch_shapes=[pltpu.VMEM(s, F32) if isinstance(s, tuple) else s for s in scratch],
-        compiler_params=pltpu.CompilerParams(vmem_limit_bytes=16 << 20),
+        compiler_params=pltpu.CompilerParams(vmem_limit_bytes=limit),
     )(*ins)
 
 
 def body(density, fields, bins, owner, species, rate_matrix, inv_weight, formation):
-    ins = [density, fields, bins, owner.reshape(1, C), species]
-    scratch = [(16, C, Z), (C, 16, NB), (264, NB)]
-    scratch += [pltpu.VMEM(x.shape, x.dtype) for x in ins] + [pltpu.SemaphoreType.DMA((5,))]
-    (sent,) = call(bin_kernel, "bin", [(G, C, NB)], ins, scratch, pltpu.HBM)
+    dma = pltpu.SemaphoreType.DMA
+    ins = [bins, fields, density, species, owner.reshape(1, C)]
+    ins += [rate_matrix, inv_weight.reshape(1, NS), formation.reshape(1, NS)]
+    sent, consts = call(
+        bin_kernel,
+        "bin",
+        [(G, C, NB), (NS, NB)],
+        ins,
+        [pltpu.VMEM(x.shape, x.dtype) for x in ins]
+        + [(2, 48 * C, NB), (16 * C, NB), (264, NB), (C, Z), (G, C, NB), (NS, NB), dma((8,)), dma((G + 1,))],
+        pl.ANY,
+        pl.ANY,
+        (64 << 20) - (64 << 10),
+    )
     got = lax.all_to_all(sent, "span", 0, 0, tiled=True)
-    sent, halo = call(column_kernel, "column", [(G // 2, R2, NB), (2, C, NB)], [got])
+    sent, halo = call(column_kernel, "column", [(G // 2, R2, NB), (2, C, NB)], [got.reshape(G * C, NB)])
     groups = [list(range(core, G, 2)) for core in range(2)]
     got = lax.all_to_all(sent, "sec", 0, 0, axis_index_groups=groups, tiled=True)
     other = lax.ppermute(got, "sec", [(i, i ^ 1) for i in range(G)])
     (sent,) = call(
         section_kernel,
         "section",
-        [(G, 8, NB)],
-        [got, other, rate_matrix, inv_weight.reshape(1, NS), formation.reshape(1, NS)],
+        [(NB, NB)],
+        [got, other, consts],
         [(NB, SECT), (2, NB, NB)],
     )
-    got = lax.all_to_all(sent, "span", 0, 0, tiled=True)
-    return call(
-        cell_kernel,
-        "cell",
-        [(1, NS, NB), (C, Z), (4, C, Z)],
-        [got, halo, fields, bins],
-    )
+    got = lax.all_to_all(sent.reshape(G, 8, NB), "span", 0, 0, tiled=True)
+    outs = [(1, NS, NB), (C, Z), (4, C, Z)]
+    return call(cell_kernel, "cell", outs, [got, halo, fields, bins], outs + [dma((6,))], to=pl.ANY)
 
 
 def solution(mesh):

time: 61.1 us -> 56.4 us (0.923)
  local copies, waits for them, and re-layouts: 4.42 us -> 0.02 us
    all_to_all x0 -> x1, blocking collectives: none -> 10.7 us  [body(): got = lax.all_to_all(sent.reshape(G, 8, NB), 'span', 0, 0, tiled=True)]
    all_to_all x2 -> x1, blocking collectives: 30 us -> 19.5 us  [body(): got = lax.all_to_all(sent, 'span', 0, 0, tiled=True)]
    unnamed x20 -> x6, local copies, waits for them, and re-layouts: 4.42 us -> 0.02 us
where the time goes in v3:
time: 56.4 us; the launch traced here: 56 us
  blocking collectives  44.3 us (79%)
  Pallas kernels  5.93 us (11%)
  starting transfers between devices  3.88 us (7%)
  waiting for transfers between devices  1.21 us (2%)
  between operations  0.68 us (1%)
    all_to_all x1, blocking collectives, body(): got = lax.all_to_all(sent, 'span', 0, 0, tiled=True)  19.5 us
    all_to_all x1, blocking collectives, body(): lax.all_to_all(sent, 'sec', 0, 0, axis_index_groups=groups, tiled=True)  14.2 us
    all_to_all x1, blocking collectives, body(): got = lax.all_to_all(sent.reshape(G, 8, NB), 'span', 0, 0, tiled=True)  10.7 us
    pallas_call x4, Pallas kernels, call(): pl.pallas_call(kernel, name=name, out_shape=[jax.ShapeDtypeStruct(s, F32)...  5.93 us
    ppermute x1, starting transfers between devices, body(): other = lax.ppermute(got, 'sec', [(i, i ^ 1) for i in range(G)])  3.88 us
    ppermute x1, waiting for transfers between devices, body(): other = lax.ppermute(got, 'sec', [(i, i ^ 1) for i in range(G)])  1.21 us
  transfers between devices with their start and end apart: 1, of which 1 were waited for; matrix products, arithmetic and copies ran while one was open for 0% of the time, Pallas kernels for 0%

profile of v3, /device:TPU:1, one launch (start us, length us, event | category | flops | bytes accessed | tf_op | source)
XLA Modules:
  0.0 56.0 jit_solution(1422674635722804274)
XLA Ops:
  0.6 2.9 %bin.1 = (f32[16,24,128]{2,1,0:T(8,128)}, f32[32,128]{1,0:T(8,128)}) custom-call(s32[24,256]{1,0:T(8,128)} %bins.1, f32[4,24,256]{2,1,0:T(8,128)} %fields.1, f32[24,256]{1,0:T(8,128)} %refs_2_.1, f32[1,32,128]{2,1,0:T(8,128)} %refs_3_.1, s32[1,24]{1,0:T(1,128)} %bitcast.7, f32[32,32]{1,0:T(8,128)} %refs_5_.1, f32[1,32]{1,0:T(1,128)} %bitcast.8, f32[1,32]{1,0:T(1,128)} %bitcast.9), custom_call_target="tpu_custom_call" | custom-call | tf_op jit(solution)/shard_map/bin/pallas_call | solution.py:312
  3.5 19.5 %all_to_all.15 = f32[16,24,128]{2,1,0:T(8,128)S(1)} all-to-all(f32[16,24,128]{2,1,0:T(8,128)} %get-tuple-element.7), channel_id=1, replica_groups=mesh['sec'=16,'span'=16] {'span'}, dimensions={0} | all-to-all | bytes 393216 | tf_op jit(solution)/shard_map/all_to_all | solution.py:338
  23.0 0.4 column.1
  23.4 0.0 copy-start.2
  23.4 14.2 %all_to_all.16.got = f32[8,72,128]{2,1,0:T(8,128)S(1)} all-to-all(f32[8,72,128]{2,1,0:T(8,128)S(1)} %get-tuple-element.8), channel_id=1, replica_groups={{0,32,64,96,128,160,192,224},{16,48,80,112,144,176,208,240},{1,33,65,97..., dimensions={0} | all-to-all | bytes 589824 | tf_op jit(solution)/shard_map/all_to_all | solution.py:341
  37.6 3.9 %collective-permute-start = (f32[8,72,128]{2,1,0:T(8,128)S(1)}, f32[8,72,128]{2,1,0:T(8,128)S(1)}, u32[]{:S(2)}, u32[]{:S(2)}) collective-permute-start(f32[8,72,128]{2,1,0:T(8,128)S(1)} %all_to_all.16.got), channel_id=1, source_target_pairs={{0,16},{16,0},{32,48},{48,32},{64,80},{80,64},{96,112},{112,96},{1... | collective-permute-start | bytes 884744 | tf_op jit(solution)/shard_map/ppermute | solution.py:342
  41.5 1.2 %collective-permute-done.other = f32[8,72,128]{2,1,0:T(8,128)S(1)} collective-permute-done((f32[8,72,128]{2,1,0:T(8,128)S(1)}, f32[8,72,128]{2,1,0:T(8,128)S(1)}, u32[]{:S(2)}, u32[]{:S(2)}) %collective-permute-start) | collective-permute-done | bytes 294944 | tf_op jit(solution)/shard_map/ppermute | solution.py:342
  42.7 0.0 copy-done.2
  42.7 1.2 %section.1 = f32[128,128]{1,0:T(8,128)S(1)} custom-call(f32[8,72,128]{2,1,0:T(8,128)S(1)} %all_to_all.16.got, f32[8,72,128]{2,1,0:T(8,128)S(1)} %collective-permute-done.other, f32[32,128]{1,0:T(8,128)S(1)} %copy-done.2), custom_call_target="tpu_custom_call" | custom-call | tf_op jit(solution)/shard_map/section/pallas_call | solution.py:312
  43.9 0.0 copy-start
  43.9 0.0 copy-start.1
  43.9 10.7 %all_to_all.17.got = f32[16,8,128]{2,1,0:T(8,128)S(1)} all-to-all(f32[16,8,128]{2,1,0:T(8,128)S(1)} %bitcast.6), channel_id=1, replica_groups=mesh['sec'=16,'span'=16] {'span'}, dimensions={0} | all-to-all | bytes 131072 | tf_op jit(solution)/shard_map/all_to_all | solution.py:350
  54.5 0.0 copy-done
  54.5 0.0 copy-done.1
  54.5 1.5 %cell.1 = (f32[1,32,128]{2,1,0:T(8,128)}, f32[24,256]{1,0:T(8,128)}, f32[4,24,256]{2,1,0:T(8,128)}) custom-call(f32[16,8,128]{2,1,0:T(8,128)S(1)} %all_to_all.17.got, f32[2,24,128]{2,1,0:T(8,128)S(1)} %get-tuple-element.10.halo, f32[4,24,256]{2,1,0:T(8,128)S(1)} %copy-done, s32[24,256]{1,0:T(8,128)S(1)} %copy-done.1), custom_call_target="tpu_custom_call" | custom-call | tf_op jit(solution)/shard_map/cell/pallas_call | solution.py:312
Async XLA Ops:
  23.4 19.3 %copy-start.2 = (f32[32,128]{1,0:T(8,128)S(1)}, f32[32,128]{1,0:T(8,128)}, u32[]{:S(2)}) copy-start(f32[32,128]{1,0:T(8,128)} %get-tuple-element.9.consts) | copy-start | bytes 49156
  37.6 5.1 %collective-permute-start = (f32[8,72,128]{2,1,0:T(8,128)S(1)}, f32[8,72,128]{2,1,0:T(8,128)S(1)}, u32[]{:S(2)}, u32[]{:S(2)}) collective-permute-start(f32[8,72,128]{2,1,0:T(8,128)S(1)} %all_to_all.16.got), channel_id=1, source_target_pairs={{0,16},{16,0},{32,48},{48,32},{64,80},{80,64},{96,112},{112,96},{1... | collective-permute-start | bytes 884744 | tf_op jit(solution)/shard_map/ppermute | solution.py:342
  43.9 10.7 %copy-start = (f32[4,24,256]{2,1,0:T(8,128)S(1)}, f32[4,24,256]{2,1,0:T(8,128)}, u32[]{:S(2)}) copy-start(f32[4,24,256]{2,1,0:T(8,128)} %fields.1) | copy-start | bytes 294916
  43.9 10.7 %copy-start.1 = (s32[24,256]{1,0:T(8,128)S(1)}, s32[24,256]{1,0:T(8,128)}, u32[]{:S(2)}) copy-start(s32[24,256]{1,0:T(8,128)} %bins.1) | copy-start | bytes 73732

commit v4 on v3

--- a/solution.py
+++ b/solution.py
@@ -40,8 +40,8 @@
 
 
 def bin_kernel(*refs):
-    ins, (sent, consts), held = refs[0:8], refs[8:10], refs[10:18]
-    vals, hist, rows, labels, out, shared, arrived, left = refs[18:26]
+    ins, (out, shared), held = refs[0:8], refs[8:10], refs[10:18]
+    vals, hist, rows, labels, arrived = refs[18:23]
     bins, fields, den, species, owner, rate_matrix, inv_weight, formation = held
     copies = [pltpu.make_async_copy(ins[n], held[n], arrived.at[n]) for n in range(8)]
     for copy in copies:
@@ -52,8 +52,6 @@
     block = jnp.concatenate([rate_matrix[...], jnp.zeros((NS, NB - NS), F32)], axis=1)
     block = jnp.where(lane == NS, column_of(inv_weight[...], NS), block)
     shared[...] = jnp.where(lane == NS + 1, column_of(formation[...], NS), block)
-    leaving = [pltpu.make_async_copy(shared, consts, left.at[G])]
-    leaving[0].start()
     lane = iota((C, Z), 1)
     d = den[...]
 
@@ -91,7 +89,7 @@
     for k in range(4):
         first, last = fields[k, :, 0:NB], fields[k, :, Z - NB : Z]
         for e, (tile, at) in enumerate(((first, 0), (first, 1), (last, NB - 2), (last, NB - 1))):
-            to = LE + 4 * e + k
+            to = LE + 4 * k + e
             edge = jnp.where(lane == to, pltpu.roll(tile, (to - at) % NB, 1), edge)
     first, last = labels[:, 0:NB], labels[:, Z - NB : Z]
     edge = jnp.where(lane == LB0, pltpu.roll(first, LB0, 1), edge)
@@ -103,23 +101,18 @@
     rows[256:264, :] = jnp.zeros((8, NB), F32)
     rows[pl.ds(4, NB, stride=2), :] = pltpu.roll(turned, LS, 1)
     rows[pl.ds(5, NB, stride=2), :] = pltpu.roll(turned, LS - 16, 1)
+    layout = [(LF + 8 * k, 0, 6 + k) for k in range(4)] + [(LC, 0, 5)] + [(LH + 10 * q, -1, q) for q in range(5)]
+    turned = [pltpu.roll(sums[q], (start - at) % NB, 1) if start != at else sums[q] for start, at, q in layout]
     for dest in range(G):
-        acc = jnp.where(lane >= LS, rows[16 * dest : 16 * dest + C, :], edge)
-        for k in range(4):
-            start = LF + 8 * k
-            moved = pltpu.roll(sums[6 + k], (start - 8 * dest) % NB, 1)
-            acc = jnp.where((lane >= start) & (lane < start + 8), moved, acc)
-        moved = pltpu.roll(sums[5], (LC - 8 * dest) % NB, 1)
-        acc = jnp.where((lane >= LC) & (lane < LC + 8), moved, acc)
-        for q in range(5):
-            start = LH + 10 * q
-            moved = pltpu.roll(sums[q], (start - 8 * dest + 1) % NB, 1)
-            acc = jnp.where((lane >= start) & (lane < start + 10), moved, acc)
+        place = lane if dest == 0 else (lane - 8 * dest) & (NB - 1)
+        acc = turned[0]
+        for n in range(1, 10):
+            acc = jnp.where(place >= layout[n][0], turned[n], acc)
+        if dest:
+            acc = pltpu.roll(acc, NB - 8 * dest, 1)
+        acc = jnp.where(lane >= LE, edge, acc)
+        acc = jnp.where(lane >= LS, rows[16 * dest : 16 * dest + C, :], acc)
         out[dest] = acc
-        leaving.append(pltpu.make_async_copy(out.at[dest], sent.at[dest], left.at[dest]))
-        leaving[-1].start()
-    for copy in leaving:
-        copy.wait()
 
 
 def column_kernel(got, out, halo):
@@ -131,10 +124,10 @@
     source, to = iota((NB, 2 * NB), 0), iota((NB, 2 * NB), 1)
     pick = jnp.where(
         to < 32,
-        LE + 12 + to // 8,
+        LE + 3 + 4 * (to // 8),
         jnp.where(
             to < 64,
-            LE + (to - 32) // 8,
+            LE + 4 * ((to - 32) // 8),
             jnp.where((to >= 128) & (to < 160), LB0, jnp.where((to >= 160) & (to < 192), LB1, -1)),
         ),
     )
@@ -162,8 +155,14 @@
         out[i, 0:C, :] = total
         for t in range(3):
             out[i, C + G * t : C + G * (t + 1), :] = tiles[t]
-    halo[0] = got[pl.ds(pl.multiple_of(C * lax.rem(me + G - 1, G), 8), C), :]
-    halo[1] = got[pl.ds(pl.multiple_of(C * lax.rem(me + 1, G), 8), C), :]
+    lane = iota((C, NB), 1)
+    left = got[pl.ds(pl.multiple_of(C * lax.rem(me + G - 1, G), 8), C), :]
+    right = got[pl.ds(pl.multiple_of(C * lax.rem(me + 1, G), 8), C), :]
+    for k in range(4):
+        first, last = pltpu.roll(right, NB - LE - 4 * k, 1), pltpu.roll(left, NB - LE - 4 * k - 4, 1)
+        halo[k] = jnp.where(lane < 2, first, jnp.where(lane >= NB - 2, last, 0.0))
+    first, last = pltpu.roll(right, NB - LB0, 1), pltpu.roll(left, NB - 1 - LB1, 1)
+    halo[4] = jnp.where(lane == 0, first, jnp.where(lane == NB - 1, last, 0.0))
 
 
 def section_kernel(got, other, consts, out, sums, turned):
@@ -177,17 +176,20 @@
     weights, heats = consts[:, NS : NS + 1], consts[:, NS + 1 : NS + 2]
     block = jnp.concatenate([consts[:, 0:NS]] * 4, axis=1)
     block = jnp.concatenate([block] * 4, axis=0)
-    block = jnp.where(iota((NB, NB), 0) // NS == iota((NB, NB), 1) // NS, block, 0.0)
+    released = jnp.sum(heats * consts[:, 0:NS], axis=0, keepdims=True)
+    block = jnp.concatenate([block, jnp.concatenate([jnp.broadcast_to(released, (8, NS))] * 4, axis=1)], axis=0)
+    row = iota((NB + 8, NB), 0)
+    block = jnp.where(jnp.where(row < NB, row // NS, row - NB) == iota((NB + 8, NB), 1) // NS, block, 0.0)
     high, mid, low = parts(block)
     blocks = [jnp.concatenate(pair, axis=1) for pair in ((high, mid), (mid, high), (low, high))]
-    first_lane = iota((NS, SECT), 1) == 0
+    not_first = iota((1, SECT), 1) > 0
 
     def rates(tile):
         high, mid, low = parts(tile)
         pairs = (high, mid), (high, mid), (high, low)
         return sum(dot(a, jnp.concatenate(b, axis=0), ((1,), (0,))) for a, b in zip(blocks, pairs))
 
-    def advance(density, moments, bin_at, current, reaction):
+    def advance(density, moments, bin_at, current, reaction, released):
         n = density.shape[0]
         weight = jnp.maximum(density, 1.0)
         cond = [m / weight for m in moments]
@@ -196,23 +198,23 @@
         rate = jnp.exp(2.0 * (1.0 - 1.0 / temp))
         mixing = 0.2 * sigmoid(cond[1])
         carried = 0.3 * sigmoid(cond[0])
-        updated, mixes, released = [], [], []
+        keep = 1.0 - 2.0 * mixing - carried
+        follow = jnp.where(not_first, carried, 0.0)
+        grow = 0.2 * rate
+        updated, mixes = [], []
         for r in range(n):
-            here = current[r + 1]
-            before = jnp.where(first_lane, 0.0, pltpu.roll(here, 1, 1))
-            react = reaction[r] * rate[r : r + 1]
+            here, row = current[r + 1], slice(r, r + 1)
             new = (
-                here
-                + mixing[r : r + 1] * (current[r + 2] + current[r] - 2.0 * here)
-                - carried[r : r + 1] * (here - before)
-                + 0.2 * react
+                keep[row] * here
+                + mixing[row] * (current[r + 2] + current[r])
+                + follow[row] * pltpu.roll(here, 1, 1)
+                + grow[row] * reaction[r]
             )
             updated.append(new)
             mixes.append(jnp.sum(weights * new * new, axis=0, keepdims=True))
-            released.append(jnp.sum(heats * react, axis=0, keepdims=True))
         mix = 1.0 + jnp.concatenate(mixes, axis=0) / NS
         rho = 1.0 / (temp * mix)
-        temp_c = temp + 0.1 * jnp.concatenate(released, axis=0) - 0.2 * sigmoid(cond[3]) * (temp - 0.5)
+        temp_c = temp + 0.1 * rate * released - 0.2 * sigmoid(cond[3]) * (temp - 0.5)
         return updated, rho, temp_c
 
     even = lax.rem(row_at, 2) == 0
@@ -228,7 +230,8 @@
     current = [tiles[b // 4][NS * (b % 4) : NS * (b % 4 + 1)] for b in range(12)]
     reaction = [reacts[b // 4][NS * (b % 4) : NS * (b % 4 + 1)] for b in range(1, 11)]
     first = [sums[LH + 10 * q : LH + 10 * (q + 1), :] for q in range(5)]
-    updated, rho, temp0 = advance(first[0], first[1:], 8 * me - 1, current, reaction)
+    released = jnp.concatenate([tile[NB : NB + 4] for tile in reacts], axis=0)[1:11]
+    updated, rho, temp0 = advance(first[0], first[1:], 8 * me - 1, current, reaction, released)
     updated[0] = jnp.where(me == 0, 0.0, updated[0])
     updated[9] = jnp.where(me == G - 1, 0.0, updated[9])
     rho, temp0 = rho[1:9], temp0[1:9]
@@ -237,7 +240,8 @@
     moments[2] = 0.7 * moments[2] + 0.3 * rho * temp0 * count
     reacts = [rates(jnp.concatenate(updated[1 + 4 * t : 5 + 4 * t], axis=0)) for t in range(2)]
     reaction = [reacts[b // 4][NS * (b % 4) : NS * (b % 4 + 1)] for b in range(8)]
-    final, rho, temp1 = advance(rho * count, moments, 8 * me, updated, reaction)
+    released = jnp.concatenate([tile[NB : NB + 4] for tile in reacts], axis=0)
+    final, rho, temp1 = advance(rho * count, moments, 8 * me, updated, reaction, released)
 
     own = got[row_at // 2, 0:C, LOWN : LOWN + 1]
     own = jnp.concatenate([own] * 3 + [jnp.full((NB - 3 * C, 1), -1.0, F32)], axis=0)
@@ -273,42 +277,37 @@
     def look(tab, index):
         return jnp.take_along_axis(tab, index, axis=1)
 
-    def cells(tab):
-        return jnp.concatenate([look(tab, bins[:, 0:NB]), look(tab, bins[:, NB:Z])], axis=1)
-
-    density_out[...] = cells(rho)
+    index = [bins[:, 0:NB], bins[:, NB:Z], halo[4].astype(jnp.int32)]
+    first, last = iota((C, NB), 1) == 0, iota((C, NB), 1) == NB - 1
+
+    def diffused(tiles):
+        up, down = [pltpu.roll(t, 1, 1) for t in tiles], [pltpu.roll(t, NB - 1, 1) for t in tiles]
+        return [
+            t + 0.2 * (jnp.where(first, up[n - 1], up[n]) + jnp.where(last, down[(n + 1) % 3], down[n]) - 2.0 * t)
+            for n, t in enumerate(tiles)
+        ]
+
+    def relaxed(tiles, tab):
+        return [t + 0.3 * (look(tab, i) - t) for t, i in zip(tiles, index)]
+
+    for h in range(2):
+        density_out[:, NB * h : NB * (h + 1)] = look(rho, index[h])
     leave(density_out, density_to)
-    lane = iota((C, Z), 1)
-    left, right = halo[0], halo[1]
-
-    def shifted(f, before, after):
-        return jnp.where(lane == 0, before, pltpu.roll(f, 1, 1)) + jnp.where(
-            lane == Z - 1, after, pltpu.roll(f, Z - 1, 1)
-        )
-
     for k in (2, 0, 1, 3):
-        f = fields[k]
-        l1, l2 = left[:, LE + 12 + k : LE + 13 + k], left[:, LE + 8 + k : LE + 9 + k]
-        r1, r2 = right[:, LE + k : LE + 1 + k], right[:, LE + 4 + k : LE + 5 + k]
-        new = f + 0.2 * (shifted(f, l1, r1) - 2.0 * f)
-        new_l = l1 + 0.2 * (l2 + f[:, 0:1] - 2.0 * l1)
-        new_r = r1 + 0.2 * (f[:, Z - 1 : Z] + r2 - 2.0 * r1)
+        tiles = diffused([fields[k, :, 0:NB], fields[k, :, NB:Z], halo[k]])
         if k == 2:
-            new = new + 0.3 * (cells(temp0) - new)
-            at_l = jnp.broadcast_to(left[:, LB1 : LB1 + 1].astype(jnp.int32), (C, NB))
-            at_r = jnp.broadcast_to(right[:, LB0 : LB0 + 1].astype(jnp.int32), (C, NB))
-            new_l = new_l + 0.3 * (look(temp0, at_l)[:, 0:1] - new_l)
-            new_r = new_r + 0.3 * (look(temp0, at_r)[:, 0:1] - new_r)
-        new = new + 0.2 * (shifted(new, new_l, new_r) - 2.0 * new)
+            tiles = relaxed(tiles, temp0)
+        tiles = diffused(tiles)
         if k == 2:
-            new = new + 0.3 * (cells(temp1) - new)
-        fields_out[k] = new
+            tiles = relaxed(tiles, temp1)
+        for h in range(2):
+            fields_out[k, :, NB * h : NB * (h + 1)] = tiles[h]
         leave(fields_out.at[k], fields_to.at[k])
     for copy in leaving:
         copy.wait()
 
 
-def call(kernel, name, outs, ins, scratch=(), source=pltpu.VMEM, to=pltpu.VMEM, limit=16 << 20):
+def call(kernel, name, outs, ins, scratch=(), source=pltpu.VMEM, to=pltpu.VMEM):
     return pl.pallas_call(
         kernel,
         name=name,
@@ -316,7 +315,7 @@
         in_specs=[pl.BlockSpec(memory_space=source)] * len(ins),
         out_specs=[pl.BlockSpec(memory_space=to)] * len(outs),
         scratch_shapes=[pltpu.VMEM(s, F32) if isinstance(s, tuple) else s for s in scratch],
-        compiler_params=pltpu.CompilerParams(vmem_limit_bytes=limit),
+        compiler_params=pltpu.CompilerParams(vmem_limit_bytes=16 << 20),
     )(*ins)
 
 
@@ -328,15 +327,13 @@
         bin_kernel,
         "bin",
         [(G, C, NB), (NS, NB)],
-        ins,
+        [pltpu.with_memory_space_constraint(x, pltpu.HBM) for x in ins],
         [pltpu.VMEM(x.shape, x.dtype) for x in ins]
-        + [(2, 48 * C, NB), (16 * C, NB), (264, NB), (C, Z), (G, C, NB), (NS, NB), dma((8,)), dma((G + 1,))],
-        pl.ANY,
-        pl.ANY,
-        (64 << 20) - (64 << 10),
+        + [(2, 48 * C, NB), (16 * C, NB), (264, NB), (C, Z), dma((8,))],
+        pltpu.HBM,
     )
     got = lax.all_to_all(sent, "span", 0, 0, tiled=True)
-    sent, halo = call(column_kernel, "column", [(G // 2, R2, NB), (2, C, NB)], [got.reshape(G * C, NB)])
+    sent, halo = call(column_kernel, "column", [(G // 2, R2, NB), (5, C, NB)], [got.reshape(G * C, NB)])
     groups = [list(range(core, G, 2)) for core in range(2)]
     got = lax.all_to_all(sent, "sec", 0, 0, axis_index_groups=groups, tiled=True)
     other = lax.ppermute(got, "sec", [(i, i ^ 1) for i in range(G)])

time: 56.4 us -> 54.7 us (0.970)
  Pallas kernels: 5.93 us -> 4.55 us
    pallas_call x4, Pallas kernels: 5.93 us -> 4.55 us  [call(): pl.pallas_call(kernel, name=name, out_shape=[jax.ShapeDtypeStruct(s, F32)...]
where the time goes in v4:
time: 54.7 us; the launch traced here: 54.4 us
  blocking collectives  44.1 us (81%)
  Pallas kernels  4.55 us (8%)
  starting transfers between devices  3.89 us (7%)
  waiting for transfers between devices  1.21 us (2%)
  between operations  0.67 us (1%)
    all_to_all x1, blocking collectives, body(): got = lax.all_to_all(sent, 'span', 0, 0, tiled=True)  19.3 us
    all_to_all x1, blocking collectives, body(): lax.all_to_all(sent, 'sec', 0, 0, axis_index_groups=groups, tiled=True)  14.1 us
    all_to_all x1, blocking collectives, body(): got = lax.all_to_all(sent.reshape(G, 8, NB), 'span', 0, 0, tiled=True)  10.7 us
    pallas_call x4, Pallas kernels, call(): pl.pallas_call(kernel, name=name, out_shape=[jax.ShapeDtypeStruct(s, F32)...  4.55 us
    ppermute x1, starting transfers between devices, body(): other = lax.ppermute(got, 'sec', [(i, i ^ 1) for i in range(G)])  3.89 us
    ppermute x1, waiting for transfers between devices, body(): other = lax.ppermute(got, 'sec', [(i, i ^ 1) for i in range(G)])  1.21 us
  transfers between devices with their start and end apart: 1, of which 1 were waited for; matrix products, arithmetic and copies ran while one was open for 0% of the time, Pallas kernels for 0%

profile of v4, /device:TPU:1, one launch (start us, length us, event | category | flops | bytes accessed | tf_op | source)
XLA Modules:
  0.0 54.4 jit_solution(3221299682002414981)
XLA Ops:
  0.6 1.9 %bin.1 = (f32[16,24,128]{2,1,0:T(8,128)S(1)}, f32[32,128]{1,0:T(8,128)S(1)}) custom-call(s32[24,256]{1,0:T(8,128)} %bins.1, f32[4,24,256]{2,1,0:T(8,128)} %fields.1, f32[24,256]{1,0:T(8,128)} %refs_2_.1, f32[1,32,128]{2,1,0:T(8,128)} %refs_3_.1, s32[1,24]{1,0:T(1,128)} %bitcast.7, f32[32,32]{1,0:T(8,128)} %refs_5_.1, f32[1,32]{1,0:T(1,128)} %bitcast.8, ...), custom_call_target="tpu_custom_call" | custom-call | tf_op jit(solution)/shard_map/bin/pallas_call | solution.py:311
  2.5 19.3 %all_to_all.15 = f32[16,24,128]{2,1,0:T(8,128)S(1)} all-to-all(f32[16,24,128]{2,1,0:T(8,128)S(1)} %get-tuple-element.7), channel_id=1, replica_groups=mesh['sec'=16,'span'=16] {'span'}, dimensions={0} | all-to-all | bytes 393216 | tf_op jit(solution)/shard_map/all_to_all | solution.py:335
  21.8 0.4 column.1
  22.2 14.1 %all_to_all.16.got = f32[8,72,128]{2,1,0:T(8,128)S(1)} all-to-all(f32[8,72,128]{2,1,0:T(8,128)S(1)} %get-tuple-element.8), channel_id=1, replica_groups={{0,32,64,96,128,160,192,224},{16,48,80,112,144,176,208,240},{1,33,65,97..., dimensions={0} | all-to-all | bytes 589824 | tf_op jit(solution)/shard_map/all_to_all | solution.py:338
  36.4 3.9 %collective-permute-start = (f32[8,72,128]{2,1,0:T(8,128)S(1)}, f32[8,72,128]{2,1,0:T(8,128)S(1)}, u32[]{:S(2)}, u32[]{:S(2)}) collective-permute-start(f32[8,72,128]{2,1,0:T(8,128)S(1)} %all_to_all.16.got), channel_id=1, source_target_pairs={{0,16},{16,0},{32,48},{48,32},{64,80},{80,64},{96,112},{112,96},{1... | collective-permute-start | bytes 884744 | tf_op jit(solution)/shard_map/ppermute | solution.py:339
  40.3 1.2 %collective-permute-done.other = f32[8,72,128]{2,1,0:T(8,128)S(1)} collective-permute-done((f32[8,72,128]{2,1,0:T(8,128)S(1)}, f32[8,72,128]{2,1,0:T(8,128)S(1)}, u32[]{:S(2)}, u32[]{:S(2)}) %collective-permute-start) | collective-permute-done | bytes 294944 | tf_op jit(solution)/shard_map/ppermute | solution.py:339
  41.5 1.1 %section.1 = f32[128,128]{1,0:T(8,128)S(1)} custom-call(f32[8,72,128]{2,1,0:T(8,128)S(1)} %all_to_all.16.got, f32[8,72,128]{2,1,0:T(8,128)S(1)} %collective-permute-done.other, f32[32,128]{1,0:T(8,128)S(1)} %get-tuple-element.9.consts), custom_call_target="tpu_custom_call" | custom-call | tf_op jit(solution)/shard_map/section/pallas_call | solution.py:311
  42.6 0.0 copy-start
  42.6 0.0 copy-start.1
  42.6 10.7 %all_to_all.17.got = f32[16,8,128]{2,1,0:T(8,128)S(1)} all-to-all(f32[16,8,128]{2,1,0:T(8,128)S(1)} %bitcast.6), channel_id=1, replica_groups=mesh['sec'=16,'span'=16] {'span'}, dimensions={0} | all-to-all | bytes 131072 | tf_op jit(solution)/shard_map/all_to_all | solution.py:347
  53.3 0.0 copy-done
  53.3 0.0 copy-done.1
  53.3 1.1 %cell.1 = (f32[1,32,128]{2,1,0:T(8,128)}, f32[24,256]{1,0:T(8,128)}, f32[4,24,256]{2,1,0:T(8,128)}) custom-call(f32[16,8,128]{2,1,0:T(8,128)S(1)} %all_to_all.17.got, f32[5,24,128]{2,1,0:T(8,128)S(1)} %get-tuple-element.10.halo, f32[4,24,256]{2,1,0:T(8,128)S(1)} %copy-done, s32[24,256]{1,0:T(8,128)S(1)} %copy-done.1), custom_call_target="tpu_custom_call" | custom-call | tf_op jit(solution)/shard_map/cell/pallas_call | solution.py:311
Async XLA Ops:
  36.4 5.1 %collective-permute-start = (f32[8,72,128]{2,1,0:T(8,128)S(1)}, f32[8,72,128]{2,1,0:T(8,128)S(1)}, u32[]{:S(2)}, u32[]{:S(2)}) collective-permute-start(f32[8,72,128]{2,1,0:T(8,128)S(1)} %all_to_all.16.got), channel_id=1, source_target_pairs={{0,16},{16,0},{32,48},{48,32},{64,80},{80,64},{96,112},{112,96},{1... | collective-permute-start | bytes 884744 | tf_op jit(solution)/shard_map/ppermute | solution.py:339
  42.6 10.7 %copy-start = (f32[4,24,256]{2,1,0:T(8,128)S(1)}, f32[4,24,256]{2,1,0:T(8,128)}, u32[]{:S(2)}) copy-start(f32[4,24,256]{2,1,0:T(8,128)} %fields.1) | copy-start | bytes 294916
  42.6 10.7 %copy-start.1 = (s32[24,256]{1,0:T(8,128)S(1)}, s32[24,256]{1,0:T(8,128)}, u32[]{:S(2)}) copy-start(s32[24,256]{1,0:T(8,128)} %bins.1) | copy-start | bytes 73732

commit v5 on v4

--- a/solution.py
+++ b/solution.py
@@ -42,7 +42,7 @@
 def bin_kernel(*refs):
     ins, (out, shared), held = refs[0:8], refs[8:10], refs[10:18]
     vals, hist, rows, labels, arrived = refs[18:23]
-    bins, fields, den, species, owner, rate_matrix, inv_weight, formation = held
+    bins, den, fields, owner, species, rate_matrix, inv_weight, formation = held
     copies = [pltpu.make_async_copy(ins[n], held[n], arrived.at[n]) for n in range(8)]
     for copy in copies:
         copy.start()
@@ -165,29 +165,72 @@
     halo[4] = jnp.where(lane == 0, first, jnp.where(lane == NB - 1, last, 0.0))
 
 
-def section_kernel(got, other, consts, out, sums, turned):
-    row_at, me = lax.axis_index("sec"), lax.axis_index("span")
-    half = G // 2 * C
-    wide = jnp.concatenate([got[:, 0:C, :].reshape(half, NB), other[:, 0:C, :].reshape(half, NB)], axis=0)
-    section = iota((G * C, SECT), 1).astype(F32)
-    hot = jnp.where(wide[:, LOWN : LOWN + 1] == section, 1.0, 0.0).astype(BF16)
+def section_lane(owner, core):
+    owner = owner.astype(jnp.int32)
+    return (owner >> 5) * 16 + (owner & 15) + jnp.where(((owner >> 4) & 1) == core, 0, NB)
+
+
+def rates(blocks, tile):
+    high = tile.astype(BF16)
+    mid = (tile - high.astype(F32)).astype(BF16)
+    pair = dot(blocks[:, 0 : 2 * NB], jnp.concatenate([high, high], axis=0), ((1,), (0,)))
+    return (pair + dot(blocks[:, 0:NB], mid, ((1,), (0,))))[0 : NB + 8]
+
+
+def half_sums(got, core, blocks, species, reacts):
+    wide = got[:, 0:C, :].reshape(G // 2 * C, NB)
+    lane = section_lane(wide[:, LOWN : LOWN + 1], core)
+    hot = jnp.where(lane == iota((G // 2 * C, SECT), 1), 1.0, 0.0).astype(BF16)
     full = dot(jnp.concatenate(parts(wide.T), axis=0), hot, ((1,), (0,)))
-    sums[...] = full[0:NB] + full[NB : 2 * NB] + full[2 * NB : 3 * NB]
-    weights, heats = consts[:, NS : NS + 1], consts[:, NS + 1 : NS + 2]
+    for t in range(3):
+        tile = got[:, C + G * t : C + G * (t + 1), :].reshape(NB, NB).T
+        species[t] = tile
+        reacts[t] = rates(blocks, tile)
+    return full[0:NB] + full[NB : 2 * NB] + full[2 * NB : 3 * NB]
+
+
+def diffused(tiles):
+    first, last = iota((C, NB), 1) == 0, iota((C, NB), 1) == NB - 1
+    up, down = [pltpu.roll(t, 1, 1) for t in tiles], [pltpu.roll(t, NB - 1, 1) for t in tiles]
+    return [
+        t + 0.2 * (jnp.where(first, up[n - 1], up[n]) + jnp.where(last, down[(n + 1) % 3], down[n]) - 2.0 * t)
+        for n, t in enumerate(tiles)
+    ]
+
+
+def own_kernel(got, consts, halo, fields, sums, species, reacts, blocks, once, early):
+    for n, k in enumerate((0, 1, 3, 2)):
+        tiles = diffused([fields[k, :, 0:NB], fields[k, :, NB:Z], halo[k]])
+        if k == 2:
+            for h in range(3):
+                once[h] = tiles[h]
+            continue
+        tiles = diffused(tiles)
+        for h in range(2):
+            early[n, :, NB * h : NB * (h + 1)] = tiles[h]
     block = jnp.concatenate([consts[:, 0:NS]] * 4, axis=1)
     block = jnp.concatenate([block] * 4, axis=0)
-    released = jnp.sum(heats * consts[:, 0:NS], axis=0, keepdims=True)
+    released = jnp.sum(consts[:, NS + 1 : NS + 2] * consts[:, 0:NS], axis=0, keepdims=True)
     block = jnp.concatenate([block, jnp.concatenate([jnp.broadcast_to(released, (8, NS))] * 4, axis=1)], axis=0)
     row = iota((NB + 8, NB), 0)
     block = jnp.where(jnp.where(row < NB, row // NS, row - NB) == iota((NB + 8, NB), 1) // NS, block, 0.0)
-    high, mid, low = parts(block)
-    blocks = [jnp.concatenate(pair, axis=1) for pair in ((high, mid), (mid, high), (low, high))]
-    not_first = iota((1, SECT), 1) > 0
-
-    def rates(tile):
-        high, mid, low = parts(tile)
-        pairs = (high, mid), (high, mid), (high, low)
-        return sum(dot(a, jnp.concatenate(b, axis=0), ((1,), (0,))) for a, b in zip(blocks, pairs))
+    high, mid, _ = parts(block)
+    blocks[0 : NB + 8, 0:NB] = high
+    blocks[0 : NB + 8, NB : 2 * NB] = mid
+    blocks[NB + 8 : NB + 16, :] = jnp.zeros((8, 2 * NB), BF16)
+    core = lax.rem(lax.axis_index("sec"), 2)
+    sums[...] = half_sums(got, core, blocks, species, reacts)
+
+
+def section_kernel(got, other, consts, own_sums, own_species, own_reacts, blocks, out, sums, species, reacts, mid, turned):
+    row_at, me = lax.axis_index("sec"), lax.axis_index("span")
+    core = lax.rem(row_at, 2)
+    sums[...] = own_sums[...] + half_sums(other, core, blocks, species, reacts)
+    weights = consts[:, NS : NS + 1]
+    lane = iota((NS, NB), 1)
+    starts = (lane & 15) == 0
+    section_0 = iota((1, SECT), 1) == NB * core
+    near, far = jnp.where(core == 0, 1, NB - 15), jnp.where(core == 0, NB - 15, 1)
 
     def advance(density, moments, bin_at, current, reaction, released):
         n = density.shape[0]
@@ -199,121 +242,124 @@
         mixing = 0.2 * sigmoid(cond[1])
         carried = 0.3 * sigmoid(cond[0])
         keep = 1.0 - 2.0 * mixing - carried
-        follow = jnp.where(not_first, carried, 0.0)
+        follow = jnp.where(section_0, 0.0, carried)
         grow = 0.2 * rate
         updated, mixes = [], []
         for r in range(n):
-            here, row = current[r + 1], slice(r, r + 1)
-            new = (
-                keep[row] * here
-                + mixing[row] * (current[r + 2] + current[r])
-                + follow[row] * pltpu.roll(here, 1, 1)
-                + grow[row] * reaction[r]
+            here = current(r + 1)
+            above, below, react, row = current(r + 2), current(r), reaction(r), slice(r, r + 1)
+            before = (
+                jnp.where(starts, pltpu.roll(here[1], near, 1), pltpu.roll(here[0], 1, 1)),
+                jnp.where(starts, pltpu.roll(here[0], far, 1), pltpu.roll(here[1], 1, 1)),
             )
+            new = []
+            for h in range(2):
+                half = slice(NB * h, NB * (h + 1))
+                new.append(
+                    keep[row, half] * here[h]
+                    + mixing[row, half] * (above[h] + below[h])
+                    + follow[row, half] * before[h]
+                    + grow[row, half] * react[h]
+                )
             updated.append(new)
-            mixes.append(jnp.sum(weights * new * new, axis=0, keepdims=True))
+            mixes.append(
+                jnp.concatenate([jnp.sum(weights * x * x, axis=0, keepdims=True) for x in new], axis=1)
+            )
         mix = 1.0 + jnp.concatenate(mixes, axis=0) / NS
         rho = 1.0 / (temp * mix)
         temp_c = temp + 0.1 * rate * released - 0.2 * sigmoid(cond[3]) * (temp - 0.5)
         return updated, rho, temp_c
 
-    even = lax.rem(row_at, 2) == 0
-    tiles = []
-    for t in range(3):
-        span = slice(C + G * t, C + G * (t + 1))
-        tile = []
-        for i in range(G):
-            mine, theirs = got[i // 2, span, :], other[i // 2, span, :]
-            tile.append(jnp.where(even, mine, theirs) if i % 2 == 0 else jnp.where(even, theirs, mine))
-        tiles.append(jnp.concatenate(tile, axis=0).T)
-    reacts = [rates(tile) for tile in tiles]
-    current = [tiles[b // 4][NS * (b % 4) : NS * (b % 4 + 1)] for b in range(12)]
-    reaction = [reacts[b // 4][NS * (b % 4) : NS * (b % 4 + 1)] for b in range(1, 11)]
+    def current(b):
+        rows = slice(NS * (b % 4), NS * (b % 4 + 1))
+        return own_species[b // 4, rows, :], species[b // 4, rows, :]
+
+    def reaction(r):
+        rows = slice(NS * ((r + 1) % 4), NS * ((r + 1) % 4 + 1))
+        return own_reacts[(r + 1) // 4, rows, :], reacts[(r + 1) // 4, rows, :]
+
+    released = [[x[t, NB : NB + 4, :] for t in range(3)] for x in (own_reacts, reacts)]
+    released = jnp.concatenate([jnp.concatenate(x, axis=0)[1:11] for x in released], axis=1)
     first = [sums[LH + 10 * q : LH + 10 * (q + 1), :] for q in range(5)]
-    released = jnp.concatenate([tile[NB : NB + 4] for tile in reacts], axis=0)[1:11]
     updated, rho, temp0 = advance(first[0], first[1:], 8 * me - 1, current, reaction, released)
-    updated[0] = jnp.where(me == 0, 0.0, updated[0])
-    updated[9] = jnp.where(me == G - 1, 0.0, updated[9])
+    updated[0] = [jnp.where(me == 0, 0.0, x) for x in updated[0]]
+    updated[9] = [jnp.where(me == G - 1, 0.0, x) for x in updated[9]]
+    for r in range(10):
+        for h in range(2):
+            mid[NS * r : NS * (r + 1), NB * h : NB * (h + 1)] = updated[r][h]
     rho, temp0 = rho[1:9], temp0[1:9]
     count = sums[LC : LC + 8, :]
     moments = [rho * sums[LF + 8 * k : LF + 8 * k + 8, :] for k in range(4)]
     moments[2] = 0.7 * moments[2] + 0.3 * rho * temp0 * count
-    reacts = [rates(jnp.concatenate(updated[1 + 4 * t : 5 + 4 * t], axis=0)) for t in range(2)]
-    reaction = [reacts[b // 4][NS * (b % 4) : NS * (b % 4 + 1)] for b in range(8)]
-    released = jnp.concatenate([tile[NB : NB + 4] for tile in reacts], axis=0)
-    final, rho, temp1 = advance(rho * count, moments, 8 * me, updated, reaction, released)
-
-    own = got[row_at // 2, 0:C, LOWN : LOWN + 1]
-    own = jnp.concatenate([own] * 3 + [jnp.full((NB - 3 * C, 1), -1.0, F32)], axis=0)
-    hot = jnp.where(own == iota((NB, SECT), 1).astype(F32), 1.0, 0.0).astype(BF16)
+    later = [rates(blocks, mid[NS + NB * t : NS + NB * (t + 1), :]) for t in range(2)]
+
+    def current(b):
+        return [mid[NS * b : NS * (b + 1), NB * h : NB * (h + 1)] for h in range(2)]
+
+    def reaction(r):
+        return [later[r // 4][NS * (r % 4) : NS * (r % 4 + 1), NB * h : NB * (h + 1)] for h in range(2)]
+
+    released = jnp.concatenate([x[NB : NB + 4] for x in later], axis=0)
+    final, rho, temp1 = advance(rho * count, moments, 8 * me, current, reaction, released)
+
+    own = section_lane(got[row_at // 2, 0:C, LOWN : LOWN + 1], core)
+    own = jnp.concatenate([own] * 3 + [jnp.full((NB - 3 * C, 1), -1, jnp.int32)], axis=0)
+    hot = jnp.where(own == iota((NB, SECT), 1), 1.0, 0.0).astype(BF16)
     table = jnp.concatenate([temp0, temp1, rho], axis=0)
     full = dot(jnp.concatenate(parts(table), axis=0), hot, ((1,), (1,)))
     full = full[0:24] + full[24:48] + full[48:72]
     lane = iota((8, NB), 1)
     cells = jnp.where(lane < C, full[0:8], jnp.where(lane < 2 * C, full[8:16], full[16:24]))
     for t in range(2):
-        tile = jnp.concatenate(final[4 * t : 4 * t + 4], axis=0)
-        turned[t] = jnp.where(row_at < 8, tile[:, 0:NB], tile[:, NB:SECT]).T
+        turned[t] = jnp.concatenate([x[0] for x in final[4 * t : 4 * t + 4]], axis=0).T
     lane = iota((G, NB), 1)
-    start = pl.multiple_of(16 * lax.rem(row_at, 8), 16)
+    start = pl.multiple_of(16 * (row_at // 2), 16)
     for b in range(8):
         own_sections = turned[b // 4, pl.ds(start, G), :]
         moved = pltpu.roll(own_sections, (96 - 32 * (b % 4)) % NB, 1)
         out[pl.ds(b, G, stride=8), :] = jnp.where(lane >= 96, moved, cells[b : b + 1, :])
 
 
-def cell_kernel(got, halo, fields, bins, species_to, density_to, fields_to, species_out, density_out, fields_out, left_at):
+def cell_kernel(got, halo, bins, once, early, species_to, density_to, fields_to, species_out, density_out, field, left_at):
     leaving = []
 
     def leave(source, to):
         leaving.append(pltpu.make_async_copy(source, to, left_at.at[len(leaving)]))
         leaving[-1].start()
 
+    for n, k in enumerate((0, 1, 3)):
+        leave(early.at[n], fields_to.at[k])
     table = got[...].reshape(NB, NB).T
+    temp0, temp1, rho = table[0:C], table[C : 2 * C], table[2 * C : 3 * C]
+    index = [bins[:, 0:NB], bins[:, NB:Z], halo[4].astype(jnp.int32)]
+
+    def look(tab, index):
+        return jnp.take_along_axis(tab, index, axis=1)
+
+    def relaxed(tiles, tab):
+        return [t + 0.3 * (look(tab, i) - t) for t, i in zip(tiles, index)]
+
     species_out[0] = table[96:128]
     leave(species_out, species_to)
-    temp0, temp1, rho = table[0:C], table[C : 2 * C], table[2 * C : 3 * C]
-
-    def look(tab, index):
-        return jnp.take_along_axis(tab, index, axis=1)
-
-    index = [bins[:, 0:NB], bins[:, NB:Z], halo[4].astype(jnp.int32)]
-    first, last = iota((C, NB), 1) == 0, iota((C, NB), 1) == NB - 1
-
-    def diffused(tiles):
-        up, down = [pltpu.roll(t, 1, 1) for t in tiles], [pltpu.roll(t, NB - 1, 1) for t in tiles]
-        return [
-            t + 0.2 * (jnp.where(first, up[n - 1], up[n]) + jnp.where(last, down[(n + 1) % 3], down[n]) - 2.0 * t)
-            for n, t in enumerate(tiles)
-        ]
-
-    def relaxed(tiles, tab):
-        return [t + 0.3 * (look(tab, i) - t) for t, i in zip(tiles, index)]
-
     for h in range(2):
         density_out[:, NB * h : NB * (h + 1)] = look(rho, index[h])
     leave(density_out, density_to)
-    for k in (2, 0, 1, 3):
-        tiles = diffused([fields[k, :, 0:NB], fields[k, :, NB:Z], halo[k]])
-        if k == 2:
-            tiles = relaxed(tiles, temp0)
-        tiles = diffused(tiles)
-        if k == 2:
-            tiles = relaxed(tiles, temp1)
-        for h in range(2):
-            fields_out[k, :, NB * h : NB * (h + 1)] = tiles[h]
-        leave(fields_out.at[k], fields_to.at[k])
+    tiles = relaxed(diffused(relaxed([once[h] for h in range(3)], temp0)), temp1)
+    for h in range(2):
+        field[:, NB * h : NB * (h + 1)] = tiles[h]
+    leave(field, fields_to.at[2])
     for copy in leaving:
         copy.wait()
 
 
-def call(kernel, name, outs, ins, scratch=(), source=pltpu.VMEM, to=pltpu.VMEM):
+def call(kernel, name, outs, ins, scratch=(), source=pltpu.VMEM):
+    outs = [(pltpu.VMEM, jax.ShapeDtypeStruct(s, F32)) if isinstance(s[0], int) else s for s in outs]
     return pl.pallas_call(
         kernel,
         name=name,
-        out_shape=[jax.ShapeDtypeStruct(s, F32) for s in outs],
+        out_shape=[s if space == pltpu.VMEM else space(s.shape, s.dtype) for space, s in outs],
         in_specs=[pl.BlockSpec(memory_space=source)] * len(ins),
-        out_specs=[pl.BlockSpec(memory_space=to)] * len(outs),
+        out_specs=[pl.BlockSpec(memory_space=space) for space, _ in outs],
         scratch_shapes=[pltpu.VMEM(s, F32) if isinstance(s, tuple) else s for s in scratch],
         compiler_params=pltpu.CompilerParams(vmem_limit_bytes=16 << 20),
     )(*ins)
@@ -321,8 +367,8 @@
 
 def body(density, fields, bins, owner, species, rate_matrix, inv_weight, formation):
     dma = pltpu.SemaphoreType.DMA
-    ins = [bins, fields, density, species, owner.reshape(1, C)]
-    ins += [rate_matrix, inv_weight.reshape(1, NS), formation.reshape(1, NS)]
+    ins = [bins, density, fields, owner.reshape(1, C)]
+    ins += [species, rate_matrix, inv_weight.reshape(1, NS), formation.reshape(1, NS)]
     sent, consts = call(
         bin_kernel,
         "bin",
@@ -337,16 +383,17 @@
     groups = [list(range(core, G, 2)) for core in range(2)]
     got = lax.all_to_all(sent, "sec", 0, 0, axis_index_groups=groups, tiled=True)
     other = lax.ppermute(got, "sec", [(i, i ^ 1) for i in range(G)])
-    (sent,) = call(
-        section_kernel,
-        "section",
-        [(NB, NB)],
-        [got, other, consts],
-        [(NB, SECT), (2, NB, NB)],
+    halves = [(NB, SECT), (3, NB, NB), (3, NB + 8, NB)]
+    blocks = (pltpu.VMEM, jax.ShapeDtypeStruct((NB + 16, 2 * NB), BF16))
+    far = [(pltpu.HBM, jax.ShapeDtypeStruct(s, F32)) for s in ((1, NS, NB), (C, Z), (4, C, Z))]
+    *own, once, early = call(
+        own_kernel, "own", halves + [blocks, (3, C, NB), (3, C, Z)], [got, consts, halo, fields]
     )
+    scratch = halves + [(10 * NS, SECT), (2, NB, NB)]
+    (sent,) = call(section_kernel, "section", [(NB, NB)], [got, other, consts] + own, scratch)
     got = lax.all_to_all(sent.reshape(G, 8, NB), "span", 0, 0, tiled=True)
-    outs = [(1, NS, NB), (C, Z), (4, C, Z)]
-    return call(cell_kernel, "cell", outs, [got, halo, fields, bins], outs + [dma((6,))], to=pl.ANY)
+    scratch = [(1, NS, NB), (C, Z), (C, Z), dma((6,))]
+    return call(cell_kernel, "cell", far, [got, halo, bins, once, early], scratch)
 
 
 def solution(mesh):

time: 54.7 us -> 54.4 us (level)
    pallas_call x4 -> x5, Pallas kernels: 4.55 us -> 4.68 us  [call(): pl.pallas_call(kernel, name=name, out_shape=[s if space == pltpu.VMEM els...]
  transfers between devices with their start and end apart: 1 -> 1, of which waited for: 1 -> 1; matrix products, arithmetic and copies ran while one was open for 0% -> 0% of each run, Pallas kernels for 0% -> 1%
where the time goes in v5:
time: 54.4 us; the launch traced here: 54.1 us
  blocking collectives  44.1 us (81%)
  Pallas kernels  4.68 us (9%)
  starting transfers between devices  3.89 us (7%)
  waiting for transfers between devices  0.72 us (1%)
  between operations  0.68 us (1%)
    all_to_all x1, blocking collectives, body(): got = lax.all_to_all(sent, 'span', 0, 0, tiled=True)  19.3 us
    all_to_all x1, blocking collectives, body(): lax.all_to_all(sent, 'sec', 0, 0, axis_index_groups=groups, tiled=True)  14.3 us
    all_to_all x1, blocking collectives, body(): got = lax.all_to_all(sent.reshape(G, 8, NB), 'span', 0, 0, tiled=True)  10.5 us
    pallas_call x5, Pallas kernels, call(): pl.pallas_call(kernel, name=name, out_shape=[s if space == pltpu.VMEM els...  4.68 us
    ppermute x1, starting transfers between devices, body(): other = lax.ppermute(got, 'sec', [(i, i ^ 1) for i in range(G)])  3.89 us
  transfers between devices with their start and end apart: 1, of which 1 were waited for; matrix products, arithmetic and copies ran while one was open for 0% of the time, Pallas kernels for 1%

profile of v5, /device:TPU:1, one launch (start us, length us, event | category | flops | bytes accessed | tf_op | source)
XLA Modules:
  0.0 54.1 jit_solution(14964798165140488446)
XLA Ops:
  0.6 1.9 %bin.1 = (f32[16,24,128]{2,1,0:T(8,128)S(1)}, f32[32,128]{1,0:T(8,128)S(1)}) custom-call(s32[24,256]{1,0:T(8,128)} %bins.1, f32[24,256]{1,0:T(8,128)} %refs_1_.1, f32[4,24,256]{2,1,0:T(8,128)} %fields.1, s32[1,24]{1,0:T(1,128)} %bitcast.7, f32[1,32,128]{2,1,0:T(8,128)} %refs_4_.1, f32[32,32]{1,0:T(8,128)} %refs_5_.1, f32[1,32]{1,0:T(1,128)} %bitcast.8, ...), custom_call_target="tpu_custom_call" | custom-call | tf_op jit(solution)/shard_map/bin/pallas_call | solution.py:357
  2.5 19.3 %all_to_all.15 = f32[16,24,128]{2,1,0:T(8,128)S(1)} all-to-all(f32[16,24,128]{2,1,0:T(8,128)S(1)} %get-tuple-element.13), channel_id=1, replica_groups=mesh['sec'=16,'span'=16] {'span'}, dimensions={0} | all-to-all | bytes 393216 | tf_op jit(solution)/shard_map/all_to_all | solution.py:381
  21.8 0.4 column.1
  22.2 0.0 copy-start
  22.3 14.3 %all_to_all.16.got = f32[8,72,128]{2,1,0:T(8,128)S(1)} all-to-all(f32[8,72,128]{2,1,0:T(8,128)S(1)} %get-tuple-element.14), channel_id=1, replica_groups={{0,32,64,96,128,160,192,224},{16,48,80,112,144,176,208,240},{1,33,65,97..., dimensions={0} | all-to-all | bytes 589824 | tf_op jit(solution)/shard_map/all_to_all | solution.py:384
  36.5 3.9 %collective-permute-start = (f32[8,72,128]{2,1,0:T(8,128)S(1)}, f32[8,72,128]{2,1,0:T(8,128)S(1)}, u32[]{:S(2)}, u32[]{:S(2)}) collective-permute-start(f32[8,72,128]{2,1,0:T(8,128)S(1)} %all_to_all.16.got), channel_id=1, source_target_pairs={{0,16},{16,0},{32,48},{48,32},{64,80},{80,64},{96,112},{112,96},{1... | collective-permute-start | bytes 884744 | tf_op jit(solution)/shard_map/ppermute | solution.py:385
  40.4 0.0 copy-done
  40.4 0.5 own.1
  40.9 0.7 %collective-permute-done.other = f32[8,72,128]{2,1,0:T(8,128)S(1)} collective-permute-done((f32[8,72,128]{2,1,0:T(8,128)S(1)}, f32[8,72,128]{2,1,0:T(8,128)S(1)}, u32[]{:S(2)}, u32[]{:S(2)}) %collective-permute-start) | collective-permute-done | bytes 294944 | tf_op jit(solution)/shard_map/ppermute | solution.py:385
  41.6 1.0 %section.1 = f32[128,128]{1,0:T(8,128)S(1)} custom-call(f32[8,72,128]{2,1,0:T(8,128)S(1)} %all_to_all.16.got, f32[8,72,128]{2,1,0:T(8,128)S(1)} %collective-permute-done.other, f32[32,128]{1,0:T(8,128)S(1)} %get-tuple-element.15.consts, f32[128,256]{1,0:T(8,128)S(1)} %get-tuple-element.17.own_sums, f32[3,128,128]{2,1,0:T(8,128)S(1)} %get-tuple-element.18.own_species, ...), custom_call_target="tpu_custom_call" | custom-call | tf_op jit(solution)/shard_map/section/pallas_call | solution.py:357
  42.6 0.0 copy-start.1
  42.6 10.5 %all_to_all.17.got = f32[16,8,128]{2,1,0:T(8,128)S(1)} all-to-all(f32[16,8,128]{2,1,0:T(8,128)S(1)} %bitcast.6), channel_id=1, replica_groups=mesh['sec'=16,'span'=16] {'span'}, dimensions={0} | all-to-all | bytes 131072 | tf_op jit(solution)/shard_map/all_to_all | solution.py:394
  53.1 0.0 copy-done.1
  53.1 0.9 %cell.1 = (f32[1,32,128]{2,1,0:T(8,128)}, f32[24,256]{1,0:T(8,128)}, f32[4,24,256]{2,1,0:T(8,128)}) custom-call(f32[16,8,128]{2,1,0:T(8,128)S(1)} %all_to_all.17.got, f32[5,24,128]{2,1,0:T(8,128)S(1)} %get-tuple-element.16.halo, s32[24,256]{1,0:T(8,128)S(1)} %copy-done.1, f32[3,24,128]{2,1,0:T(8,128)S(1)} %get-tuple-element.21.once, ...), custom_call_target="tpu_custom_call" | custom-call | tf_op jit(solution)/shard_map/cell/pallas_call | solution.py:357
Async XLA Ops:
  22.2 18.2 %copy-start = (f32[4,24,256]{2,1,0:T(8,128)S(1)}, f32[4,24,256]{2,1,0:T(8,128)}, u32[]{:S(2)}) copy-start(f32[4,24,256]{2,1,0:T(8,128)} %fields.1) | copy-start | bytes 294916
  36.5 5.1 %collective-permute-start = (f32[8,72,128]{2,1,0:T(8,128)S(1)}, f32[8,72,128]{2,1,0:T(8,128)S(1)}, u32[]{:S(2)}, u32[]{:S(2)}) collective-permute-start(f32[8,72,128]{2,1,0:T(8,128)S(1)} %all_to_all.16.got), channel_id=1, source_target_pairs={{0,16},{16,0},{32,48},{48,32},{64,80},{80,64},{96,112},{112,96},{1... | collective-permute-start | bytes 884744 | tf_op jit(solution)/shard_map/ppermute | solution.py:385
  42.6 10.5 %copy-start.1 = (s32[24,256]{1,0:T(8,128)S(1)}, s32[24,256]{1,0:T(8,128)}, u32[]{:S(2)}) copy-start(s32[24,256]{1,0:T(8,128)} %bins.1) | copy-start | bytes 73732

commit v6 on v5

--- a/solution.py
+++ b/solution.py
@@ -43,9 +43,27 @@
     ins, (out, shared), held = refs[0:8], refs[8:10], refs[10:18]
     vals, hist, rows, labels, arrived = refs[18:23]
     bins, den, fields, owner, species, rate_matrix, inv_weight, formation = held
-    copies = [pltpu.make_async_copy(ins[n], held[n], arrived.at[n]) for n in range(8)]
+    moves = [(ins[n], held[n]) for n in (0, 1, 3, 4, 5, 6, 7)]
+    moves += [(ins[2].at[k], held[2].at[k]) for k in range(4)]
+    copies = [pltpu.make_async_copy(source, to, arrived.at[n]) for n, (source, to) in enumerate(moves)]
     for copy in copies:
         copy.start()
+
+    def keep(q, value):
+        high, mid, low = parts(value)
+        for p, part in enumerate((high, mid, low)):
+            at = C * (16 * p + q)
+            part = part.astype(F32)
+            vals[0, at : at + C, :] = part[:, 0:NB]
+            vals[1, at : at + C, :] = part[:, NB:Z]
+
+    keep(5, jnp.ones((C, Z), F32))
+    for p in range(3):
+        at = C * (16 * p + 10)
+        for h in range(2):
+            vals[h, at : at + 6 * C, :] = jnp.zeros((6 * C, NB), F32)
+    rows[0:8, :] = jnp.zeros((8, NB), F32)
+    rows[256:264, :] = jnp.zeros((8, NB), F32)
     for copy in copies:
         copy.wait()
     lane = iota((NS, NB), 1)
@@ -55,26 +73,13 @@
     lane = iota((C, Z), 1)
     d = den[...]
 
-    def keep(q, value):
-        high, mid, low = parts(value)
-        for p, part in enumerate((high, mid, low)):
-            at = C * (16 * p + q)
-            part = part.astype(F32)
-            vals[0, at : at + C, :] = part[:, 0:NB]
-            vals[1, at : at + C, :] = part[:, NB:Z]
-
     keep(0, d)
-    keep(5, jnp.ones((C, Z), F32))
     for k in range(4):
         f = fields[k]
         before = jnp.where(lane == 0, 0.0, pltpu.roll(f, 1, 1))
         after = jnp.where(lane == Z - 1, 0.0, pltpu.roll(f, Z - 1, 1))
         keep(1 + k, d * f)
         keep(6 + k, f + 0.2 * (before + after - 2.0 * f))
-    for p in range(3):
-        at = C * (16 * p + 10)
-        for h in range(2):
-            vals[h, at : at + 6 * C, :] = jnp.zeros((6 * C, NB), F32)
     labels[...] = bins[...].astype(F32)
     which = iota((NB, Z), 0).astype(F32).astype(BF16).reshape(8, 16, Z)
     one, zero = jnp.ones((8, 16, Z), BF16), jnp.zeros((8, 16, Z), BF16)
@@ -97,8 +102,6 @@
     edge = jnp.where(lane == LOWN, column_of(owner[...].astype(F32), C), edge)
     sums = [hist[pl.ds(q, C, stride=16), :] for q in range(10)]
     turned = jnp.concatenate([species[0], jnp.zeros((NB - NS, NB), F32)], axis=0).T
-    rows[0:8, :] = jnp.zeros((8, NB), F32)
-    rows[256:264, :] = jnp.zeros((8, NB), F32)
     rows[pl.ds(4, NB, stride=2), :] = pltpu.roll(turned, LS, 1)
     rows[pl.ds(5, NB, stride=2), :] = pltpu.roll(turned, LS - 16, 1)
     layout = [(LF + 8 * k, 0, 6 + k) for k in range(4)] + [(LC, 0, 5)] + [(LH + 10 * q, -1, q) for q in range(5)]
@@ -222,7 +225,7 @@
     sums[...] = half_sums(got, core, blocks, species, reacts)
 
 
-def section_kernel(got, other, consts, own_sums, own_species, own_reacts, blocks, out, sums, species, reacts, mid, turned):
+def section_kernel(got, other, consts, own_sums, own_species, own_reacts, blocks, out, sums, species, reacts, mid, turned, rows_of):
     row_at, me = lax.axis_index("sec"), lax.axis_index("span")
     core = lax.rem(row_at, 2)
     sums[...] = own_sums[...] + half_sums(other, core, blocks, species, reacts)
@@ -232,8 +235,9 @@
     section_0 = iota((1, SECT), 1) == NB * core
     near, far = jnp.where(core == 0, 1, NB - 15), jnp.where(core == 0, NB - 15, 1)
 
-    def advance(density, moments, bin_at, current, reaction, released):
+    def advance(density, moments, bin_at, current, reaction, released, put):
         n = density.shape[0]
+        inner = slice(1, 9) if n == 10 else slice(0, 8)
         weight = jnp.maximum(density, 1.0)
         cond = [m / weight for m in moments]
         eta = ((bin_at + iota((n, SECT), 0)).astype(F32) + 0.5) / NB
@@ -241,13 +245,13 @@
         rate = jnp.exp(2.0 * (1.0 - 1.0 / temp))
         mixing = 0.2 * sigmoid(cond[1])
         carried = 0.3 * sigmoid(cond[0])
-        keep = 1.0 - 2.0 * mixing - carried
         follow = jnp.where(section_0, 0.0, carried)
-        grow = 0.2 * rate
-        updated, mixes = [], []
+        for c, coefficient in enumerate((1.0 - 2.0 * mixing - carried, mixing, follow, 0.2 * rate)):
+            rows_of[16 * c : 16 * c + n, :] = coefficient
+        mixes = []
         for r in range(n):
             here = current(r + 1)
-            above, below, react, row = current(r + 2), current(r), reaction(r), slice(r, r + 1)
+            above, below, react = current(r + 2), current(r), reaction(r)
             before = (
                 jnp.where(starts, pltpu.roll(here[1], near, 1), pltpu.roll(here[0], 1, 1)),
                 jnp.where(starts, pltpu.roll(here[0], far, 1), pltpu.roll(here[1], 1, 1)),
@@ -255,20 +259,18 @@
             new = []
             for h in range(2):
                 half = slice(NB * h, NB * (h + 1))
-                new.append(
-                    keep[row, half] * here[h]
-                    + mixing[row, half] * (above[h] + below[h])
-                    + follow[row, half] * before[h]
-                    + grow[row, half] * react[h]
+                keep, spread, follow, grow = [rows_of[16 * c + r : 16 * c + r + 1, half] for c in range(4)]
+                new.append(keep * here[h] + spread * (above[h] + below[h]) + follow * before[h] + grow * react[h])
+            put(r, new)
+            if inner.start <= r < inner.stop:
+                mixes.append(
+                    jnp.concatenate([jnp.sum(weights * x * x, axis=0, keepdims=True) for x in new], axis=1)
                 )
-            updated.append(new)
-            mixes.append(
-                jnp.concatenate([jnp.sum(weights * x * x, axis=0, keepdims=True) for x in new], axis=1)
-            )
         mix = 1.0 + jnp.concatenate(mixes, axis=0) / NS
+        temp, rate, loss = temp[inner], rate[inner], cond[3][inner]
         rho = 1.0 / (temp * mix)
-        temp_c = temp + 0.1 * rate * released - 0.2 * sigmoid(cond[3]) * (temp - 0.5)
-        return updated, rho, temp_c
+        temp_c = temp + 0.1 * rate * released - 0.2 * sigmoid(loss) * (temp - 0.5)
+        return rho, temp_c
 
     def current(b):
         rows = slice(NS * (b % 4), NS * (b % 4 + 1))
@@ -279,15 +281,16 @@
         return own_reacts[(r + 1) // 4, rows, :], reacts[(r + 1) // 4, rows, :]
 
     released = [[x[t, NB : NB + 4, :] for t in range(3)] for x in (own_reacts, reacts)]
-    released = jnp.concatenate([jnp.concatenate(x, axis=0)[1:11] for x in released], axis=1)
+    released = jnp.concatenate([jnp.concatenate(x, axis=0)[2:10] for x in released], axis=1)
     first = [sums[LH + 10 * q : LH + 10 * (q + 1), :] for q in range(5)]
-    updated, rho, temp0 = advance(first[0], first[1:], 8 * me - 1, current, reaction, released)
-    updated[0] = [jnp.where(me == 0, 0.0, x) for x in updated[0]]
-    updated[9] = [jnp.where(me == G - 1, 0.0, x) for x in updated[9]]
-    for r in range(10):
+
+    def put(r, new):
+        outside = (me == 0) if r == 0 else (me == G - 1) if r == 9 else None
         for h in range(2):
-            mid[NS * r : NS * (r + 1), NB * h : NB * (h + 1)] = updated[r][h]
-    rho, temp0 = rho[1:9], temp0[1:9]
+            value = new[h] if outside is None else jnp.where(outside, 0.0, new[h])
+            mid[NS * r : NS * (r + 1), NB * h : NB * (h + 1)] = value
+
+    rho, temp0 = advance(first[0], first[1:], 8 * me - 1, current, reaction, released, put)
     count = sums[LC : LC + 8, :]
     moments = [rho * sums[LF + 8 * k : LF + 8 * k + 8, :] for k in range(4)]
     moments[2] = 0.7 * moments[2] + 0.3 * rho * temp0 * count
@@ -300,7 +303,11 @@
         return [later[r // 4][NS * (r % 4) : NS * (r % 4 + 1), NB * h : NB * (h + 1)] for h in range(2)]
 
     released = jnp.concatenate([x[NB : NB + 4] for x in later], axis=0)
-    final, rho, temp1 = advance(rho * count, moments, 8 * me, current, reaction, released)
+
+    def put(r, new):
+        turned[r // 4, NS * (r % 4) : NS * (r % 4 + 1), :] = new[0]
+
+    rho, temp1 = advance(rho * count, moments, 8 * me, current, reaction, released, put)
 
     own = section_lane(got[row_at // 2, 0:C, LOWN : LOWN + 1], core)
     own = jnp.concatenate([own] * 3 + [jnp.full((NB - 3 * C, 1), -1, jnp.int32)], axis=0)
@@ -311,7 +318,7 @@
     lane = iota((8, NB), 1)
     cells = jnp.where(lane < C, full[0:8], jnp.where(lane < 2 * C, full[8:16], full[16:24]))
     for t in range(2):
-        turned[t] = jnp.concatenate([x[0] for x in final[4 * t : 4 * t + 4]], axis=0).T
+        turned[t] = turned[t].T
     lane = iota((G, NB), 1)
     start = pl.multiple_of(16 * (row_at // 2), 16)
     for b in range(8):
@@ -375,7 +382,7 @@
         [(G, C, NB), (NS, NB)],
         [pltpu.with_memory_space_constraint(x, pltpu.HBM) for x in ins],
         [pltpu.VMEM(x.shape, x.dtype) for x in ins]
-        + [(2, 48 * C, NB), (16 * C, NB), (264, NB), (C, Z), dma((8,))],
+        + [(2, 48 * C, NB), (16 * C, NB), (264, NB), (C, Z), dma((11,))],
         pltpu.HBM,
     )
     got = lax.all_to_all(sent, "span", 0, 0, tiled=True)
@@ -389,7 +396,7 @@
     *own, once, early = call(
         own_kernel, "own", halves + [blocks, (3, C, NB), (3, C, Z)], [got, consts, halo, fields]
     )
-    scratch = halves + [(10 * NS, SECT), (2, NB, NB)]
+    scratch = halves + [(10 * NS, SECT), (2, NB, NB), (64, SECT)]
     (sent,) = call(section_kernel, "section", [(NB, NB)], [got, other, consts] + own, scratch)
     got = lax.all_to_all(sent.reshape(G, 8, NB), "span", 0, 0, tiled=True)
     scratch = [(1, NS, NB), (C, Z), (C, Z), dma((6,))]

time: 54.4 us -> 54.4 us (level)
  no operation moved by 1% of the time
where the time goes in v6:
time: 54.4 us; the launch traced here: 54 us
  blocking collectives  44.1 us (81%)
  Pallas kernels  4.66 us (9%)
  starting transfers between devices  3.91 us (7%)
  waiting for transfers between devices  0.72 us (1%)
  between operations  0.68 us (1%)
    all_to_all x1, blocking collectives, body(): got = lax.all_to_all(sent, 'span', 0, 0, tiled=True)  19.3 us
    all_to_all x1, blocking collectives, body(): lax.all_to_all(sent, 'sec', 0, 0, axis_index_groups=groups, tiled=True)  14.2 us
    all_to_all x1, blocking collectives, body(): got = lax.all_to_all(sent.reshape(G, 8, NB), 'span', 0, 0, tiled=True)  10.5 us
    pallas_call x5, Pallas kernels, call(): pl.pallas_call(kernel, name=name, out_shape=[s if space == pltpu.VMEM els...  4.66 us
    ppermute x1, starting transfers between devices, body(): other = lax.ppermute(got, 'sec', [(i, i ^ 1) for i in range(G)])  3.91 us
  transfers between devices with their start and end apart: 1, of which 1 were waited for; matrix products, arithmetic and copies ran while one was open for 0% of the time, Pallas kernels for 1%

profile of v6, /device:TPU:1, one launch (start us, length us, event | category | flops | bytes accessed | tf_op | source)
XLA Modules:
  0.0 54.0 jit_solution(5590966387190084674)
XLA Ops:
  0.6 1.9 %bin.1 = (f32[16,24,128]{2,1,0:T(8,128)S(1)}, f32[32,128]{1,0:T(8,128)S(1)}) custom-call(s32[24,256]{1,0:T(8,128)} %bins.1, f32[24,256]{1,0:T(8,128)} %refs_1_.1, f32[4,24,256]{2,1,0:T(8,128)} %fields.1, s32[1,24]{1,0:T(1,128)} %bitcast.7, f32[1,32,128]{2,1,0:T(8,128)} %refs_4_.1, f32[32,32]{1,0:T(8,128)} %refs_5_.1, f32[1,32]{1,0:T(1,128)} %bitcast.8, ...), custom_call_target="tpu_custom_call" | custom-call | tf_op jit(solution)/shard_map/bin/pallas_call | solution.py:364
  2.5 19.3 %all_to_all.15 = f32[16,24,128]{2,1,0:T(8,128)S(1)} all-to-all(f32[16,24,128]{2,1,0:T(8,128)S(1)} %get-tuple-element.13), channel_id=1, replica_groups=mesh['sec'=16,'span'=16] {'span'}, dimensions={0} | all-to-all | bytes 393216 | tf_op jit(solution)/shard_map/all_to_all | solution.py:388
  21.8 0.4 column.1
  22.2 0.0 copy-start
  22.2 14.2 %all_to_all.16.got = f32[8,72,128]{2,1,0:T(8,128)S(1)} all-to-all(f32[8,72,128]{2,1,0:T(8,128)S(1)} %get-tuple-element.14), channel_id=1, replica_groups={{0,32,64,96,128,160,192,224},{16,48,80,112,144,176,208,240},{1,33,65,97..., dimensions={0} | all-to-all | bytes 589824 | tf_op jit(solution)/shard_map/all_to_all | solution.py:391
  36.5 3.9 %collective-permute-start = (f32[8,72,128]{2,1,0:T(8,128)S(1)}, f32[8,72,128]{2,1,0:T(8,128)S(1)}, u32[]{:S(2)}, u32[]{:S(2)}) collective-permute-start(f32[8,72,128]{2,1,0:T(8,128)S(1)} %all_to_all.16.got), channel_id=1, source_target_pairs={{0,16},{16,0},{32,48},{48,32},{64,80},{80,64},{96,112},{112,96},{1... | collective-permute-start | bytes 884744 | tf_op jit(solution)/shard_map/ppermute | solution.py:392
  40.4 0.0 copy-done
  40.4 0.5 own.1
  40.9 0.7 %collective-permute-done.other = f32[8,72,128]{2,1,0:T(8,128)S(1)} collective-permute-done((f32[8,72,128]{2,1,0:T(8,128)S(1)}, f32[8,72,128]{2,1,0:T(8,128)S(1)}, u32[]{:S(2)}, u32[]{:S(2)}) %collective-permute-start) | collective-permute-done | bytes 294944 | tf_op jit(solution)/shard_map/ppermute | solution.py:392
  41.6 0.9 %section.1 = f32[128,128]{1,0:T(8,128)S(1)} custom-call(f32[8,72,128]{2,1,0:T(8,128)S(1)} %all_to_all.16.got, f32[8,72,128]{2,1,0:T(8,128)S(1)} %collective-permute-done.other, f32[32,128]{1,0:T(8,128)S(1)} %get-tuple-element.15.consts, f32[128,256]{1,0:T(8,128)S(1)} %get-tuple-element.17.own_sums, f32[3,128,128]{2,1,0:T(8,128)S(1)} %get-tuple-element.18.own_species, ...), custom_call_target="tpu_custom_call" | custom-call | tf_op jit(solution)/shard_map/section/pallas_call | solution.py:364
  42.6 0.0 copy-start.1
  42.6 10.5 %all_to_all.17.got = f32[16,8,128]{2,1,0:T(8,128)S(1)} all-to-all(f32[16,8,128]{2,1,0:T(8,128)S(1)} %bitcast.6), channel_id=1, replica_groups=mesh['sec'=16,'span'=16] {'span'}, dimensions={0} | all-to-all | bytes 131072 | tf_op jit(solution)/shard_map/all_to_all | solution.py:401
  53.1 0.0 copy-done.1
  53.1 0.9 %cell.1 = (f32[1,32,128]{2,1,0:T(8,128)}, f32[24,256]{1,0:T(8,128)}, f32[4,24,256]{2,1,0:T(8,128)}) custom-call(f32[16,8,128]{2,1,0:T(8,128)S(1)} %all_to_all.17.got, f32[5,24,128]{2,1,0:T(8,128)S(1)} %get-tuple-element.16.halo, s32[24,256]{1,0:T(8,128)S(1)} %copy-done.1, f32[3,24,128]{2,1,0:T(8,128)S(1)} %get-tuple-element.21.once, ...), custom_call_target="tpu_custom_call" | custom-call | tf_op jit(solution)/shard_map/cell/pallas_call | solution.py:364
Async XLA Ops:
  22.2 18.2 %copy-start = (f32[4,24,256]{2,1,0:T(8,128)S(1)}, f32[4,24,256]{2,1,0:T(8,128)}, u32[]{:S(2)}) copy-start(f32[4,24,256]{2,1,0:T(8,128)} %fields.1) | copy-start | bytes 294916
  36.5 5.1 %collective-permute-start = (f32[8,72,128]{2,1,0:T(8,128)S(1)}, f32[8,72,128]{2,1,0:T(8,128)S(1)}, u32[]{:S(2)}, u32[]{:S(2)}) collective-permute-start(f32[8,72,128]{2,1,0:T(8,128)S(1)} %all_to_all.16.got), channel_id=1, source_target_pairs={{0,16},{16,0},{32,48},{48,32},{64,80},{80,64},{96,112},{112,96},{1... | collective-permute-start | bytes 884744 | tf_op jit(solution)/shard_map/ppermute | solution.py:392
  42.6 10.5 %copy-start.1 = (s32[24,256]{1,0:T(8,128)S(1)}, s32[24,256]{1,0:T(8,128)}, u32[]{:S(2)}) copy-start(s32[24,256]{1,0:T(8,128)} %bins.1) | copy-start | bytes 73732

commit v7 on v6

--- a/solution.py
+++ b/solution.py
@@ -346,15 +346,15 @@
     def relaxed(tiles, tab):
         return [t + 0.3 * (look(tab, i) - t) for t, i in zip(tiles, index)]
 
+    tiles = relaxed(diffused(relaxed([once[h] for h in range(3)], temp0)), temp1)
+    for h in range(2):
+        field[:, NB * h : NB * (h + 1)] = tiles[h]
+    leave(field, fields_to.at[2])
     species_out[0] = table[96:128]
     leave(species_out, species_to)
     for h in range(2):
         density_out[:, NB * h : NB * (h + 1)] = look(rho, index[h])
     leave(density_out, density_to)
-    tiles = relaxed(diffused(relaxed([once[h] for h in range(3)], temp0)), temp1)
-    for h in range(2):
-        field[:, NB * h : NB * (h + 1)] = tiles[h]
-    leave(field, fields_to.at[2])
     for copy in leaving:
         copy.wait()
 

time: 54.4 us -> 54.4 us (level)
  no operation moved by 1% of the time
where the time goes in v7:
time: 54.4 us; the launch traced here: 54 us
  blocking collectives  44.1 us (81%)
  Pallas kernels  4.66 us (9%)
  starting transfers between devices  3.91 us (7%)
  waiting for transfers between devices  0.72 us (1%)
  between operations  0.68 us (1%)
    all_to_all x1, blocking collectives, body(): got = lax.all_to_all(sent, 'span', 0, 0, tiled=True)  19.3 us
    all_to_all x1, blocking collectives, body(): lax.all_to_all(sent, 'sec', 0, 0, axis_index_groups=groups, tiled=True)  14.2 us
    all_to_all x1, blocking collectives, body(): got = lax.all_to_all(sent.reshape(G, 8, NB), 'span', 0, 0, tiled=True)  10.5 us
    pallas_call x5, Pallas kernels, call(): pl.pallas_call(kernel, name=name, out_shape=[s if space == pltpu.VMEM els...  4.66 us
    ppermute x1, starting transfers between devices, body(): other = lax.ppermute(got, 'sec', [(i, i ^ 1) for i in range(G)])  3.91 us
  transfers between devices with their start and end apart: 1, of which 1 were waited for; matrix products, arithmetic and copies ran while one was open for 0% of the time, Pallas kernels for 1%

profile of v7, /device:TPU:1, one launch (start us, length us, event | category | flops | bytes accessed | tf_op | source)
XLA Modules:
  0.0 54.0 jit_solution(9845685631731683629)
XLA Ops:
  0.6 1.9 %bin.1 = (f32[16,24,128]{2,1,0:T(8,128)S(1)}, f32[32,128]{1,0:T(8,128)S(1)}) custom-call(s32[24,256]{1,0:T(8,128)} %bins.1, f32[24,256]{1,0:T(8,128)} %refs_1_.1, f32[4,24,256]{2,1,0:T(8,128)} %fields.1, s32[1,24]{1,0:T(1,128)} %bitcast.7, f32[1,32,128]{2,1,0:T(8,128)} %refs_4_.1, f32[32,32]{1,0:T(8,128)} %refs_5_.1, f32[1,32]{1,0:T(1,128)} %bitcast.8, ...), custom_call_target="tpu_custom_call" | custom-call | tf_op jit(solution)/shard_map/bin/pallas_call | solution.py:364
  2.5 19.3 %all_to_all.15 = f32[16,24,128]{2,1,0:T(8,128)S(1)} all-to-all(f32[16,24,128]{2,1,0:T(8,128)S(1)} %get-tuple-element.13), channel_id=1, replica_groups=mesh['sec'=16,'span'=16] {'span'}, dimensions={0} | all-to-all | bytes 393216 | tf_op jit(solution)/shard_map/all_to_all | solution.py:388
  21.8 0.4 column.1
  22.2 0.0 copy-start
  22.2 14.2 %all_to_all.16.got = f32[8,72,128]{2,1,0:T(8,128)S(1)} all-to-all(f32[8,72,128]{2,1,0:T(8,128)S(1)} %get-tuple-element.14), channel_id=1, replica_groups={{0,32,64,96,128,160,192,224},{16,48,80,112,144,176,208,240},{1,33,65,97..., dimensions={0} | all-to-all | bytes 589824 | tf_op jit(solution)/shard_map/all_to_all | solution.py:391
  36.5 3.9 %collective-permute-start = (f32[8,72,128]{2,1,0:T(8,128)S(1)}, f32[8,72,128]{2,1,0:T(8,128)S(1)}, u32[]{:S(2)}, u32[]{:S(2)}) collective-permute-start(f32[8,72,128]{2,1,0:T(8,128)S(1)} %all_to_all.16.got), channel_id=1, source_target_pairs={{0,16},{16,0},{32,48},{48,32},{64,80},{80,64},{96,112},{112,96},{1... | collective-permute-start | bytes 884744 | tf_op jit(solution)/shard_map/ppermute | solution.py:392
  40.4 0.0 copy-done
  40.4 0.5 own.1
  40.9 0.7 %collective-permute-done.other = f32[8,72,128]{2,1,0:T(8,128)S(1)} collective-permute-done((f32[8,72,128]{2,1,0:T(8,128)S(1)}, f32[8,72,128]{2,1,0:T(8,128)S(1)}, u32[]{:S(2)}, u32[]{:S(2)}) %collective-permute-start) | collective-permute-done | bytes 294944 | tf_op jit(solution)/shard_map/ppermute | solution.py:392
  41.6 0.9 %section.1 = f32[128,128]{1,0:T(8,128)S(1)} custom-call(f32[8,72,128]{2,1,0:T(8,128)S(1)} %all_to_all.16.got, f32[8,72,128]{2,1,0:T(8,128)S(1)} %collective-permute-done.other, f32[32,128]{1,0:T(8,128)S(1)} %get-tuple-element.15.consts, f32[128,256]{1,0:T(8,128)S(1)} %get-tuple-element.17.own_sums, f32[3,128,128]{2,1,0:T(8,128)S(1)} %get-tuple-element.18.own_species, ...), custom_call_target="tpu_custom_call" | custom-call | tf_op jit(solution)/shard_map/section/pallas_call | solution.py:364
  42.6 0.0 copy-start.1
  42.6 10.5 %all_to_all.17.got = f32[16,8,128]{2,1,0:T(8,128)S(1)} all-to-all(f32[16,8,128]{2,1,0:T(8,128)S(1)} %bitcast.6), channel_id=1, replica_groups=mesh['sec'=16,'span'=16] {'span'}, dimensions={0} | all-to-all | bytes 131072 | tf_op jit(solution)/shard_map/all_to_all | solution.py:401
  53.1 0.0 copy-done.1
  53.1 0.9 %cell.1 = (f32[1,32,128]{2,1,0:T(8,128)}, f32[24,256]{1,0:T(8,128)}, f32[4,24,256]{2,1,0:T(8,128)}) custom-call(f32[16,8,128]{2,1,0:T(8,128)S(1)} %all_to_all.17.got, f32[5,24,128]{2,1,0:T(8,128)S(1)} %get-tuple-element.16.halo, s32[24,256]{1,0:T(8,128)S(1)} %copy-done.1, f32[3,24,128]{2,1,0:T(8,128)S(1)} %get-tuple-element.21.once, ...), custom_call_target="tpu_custom_call" | custom-call | tf_op jit(solution)/shard_map/cell/pallas_call | solution.py:364
Async XLA Ops:
  22.2 18.2 %copy-start = (f32[4,24,256]{2,1,0:T(8,128)S(1)}, f32[4,24,256]{2,1,0:T(8,128)}, u32[]{:S(2)}) copy-start(f32[4,24,256]{2,1,0:T(8,128)} %fields.1) | copy-start | bytes 294916
  36.5 5.1 %collective-permute-start = (f32[8,72,128]{2,1,0:T(8,128)S(1)}, f32[8,72,128]{2,1,0:T(8,128)S(1)}, u32[]{:S(2)}, u32[]{:S(2)}) collective-permute-start(f32[8,72,128]{2,1,0:T(8,128)S(1)} %all_to_all.16.got), channel_id=1, source_target_pairs={{0,16},{16,0},{32,48},{48,32},{64,80},{80,64},{96,112},{112,96},{1... | collective-permute-start | bytes 884744 | tf_op jit(solution)/shard_map/ppermute | solution.py:392
  42.6 10.5 %copy-start.1 = (s32[24,256]{1,0:T(8,128)S(1)}, s32[24,256]{1,0:T(8,128)}, u32[]{:S(2)}) copy-start(s32[24,256]{1,0:T(8,128)} %bins.1) | copy-start | bytes 73732
